TPU v7x, 32 devices: a whole 2x2x4 slice. The times are simulated.
32 devices in a mesh: groups: 2 (over y), stripe: 8 (over z, x), exp: 2 (over core).
Axes of the slice: x: 2, y: 2, z: 4, core: 2. Of those that a mesh axis runs over, the one named last changes fastest.
Arguments:
- template: float32 [256, 2048], P(('groups', 'stripe'), 'exp'), parts along dimension 0, may hold values from -6 to 6
- exposure: float32 [4, 128, 2048], P(('groups', 'exp'), 'stripe'), parts along dimension 0, may hold values from -30 to 30
- cosmic_mask: int32 [4, 128, 2048], P(('groups', 'exp'), 'stripe'), parts along dimension 0, may hold values 0 or 1
- stamp_blocks: int32 [16, 16], P(('groups', 'stripe')), parts along dimension 0, may hold values from 0 to 31, as said below
- row_filters: float32 [19, 19], replicated, may hold values from -1 to 2.5
- col_filters: float32 [19, 19], replicated, may hold values from -1 to 2.5
Outputs:
- filtered: float32 [4, 128, 2048], P(('groups', 'exp'), 'stripe'), parts along dimension 0
- coefficients: float32 [4, 64], P(('groups', 'exp')), parts along dimension 0
There are 2 independent parts, one for each index of `groups`. A program takes and returns all parts, laid end to end along the dimension named above; an argument that names none is the same for every part. Nothing has to cross between parts.
Inputs may be any that keep to these rules, and one draw needn't show every extreme that they name: `stamp_blocks`: each row lists the stamps of one stripe; stamp j lies in column block 2 j or 2 j + 1.
All inputs are finite; a program needn't handle non-finite values. No bound on the sum of `cosmic_mask` on one device may be relied on, other than what follows from the above.
Results may differ from a plain program's by a relative error of at most 0.0003.
Values sent between devices are 32-bit elements; how exact they have to be, the bound alone decides.
A program may use at most 64 MiB of HBM per device.

v0:
```python
import functools

import jax
import jax.numpy as jnp
from jax import lax
from jax.experimental import pallas as pl
from jax.experimental.pallas import tpu as pltpu
from jax.sharding import PartitionSpec as P

HALF = 9
STAMP_W = 64
EDGE = 128
HIGHEST = lax.Precision.HIGHEST
MESH = pl.DeviceIdType.MESH


def round_up(n, m):
    return -(-n // m) * m


def row_coords(first, count, region_rows):
    index = lax.broadcasted_iota(jnp.int32, (count, 1), 0).astype(jnp.float32) + first
    return (2.0 * index + 1.0) / region_rows - 1.0


def col_coords(first, count, col_total):
    index = lax.broadcasted_iota(jnp.int32, (1, count), 1).astype(jnp.float32) + first
    return (2.0 * index + 1.0) / col_total - 1.0


def background(u, v):
    uu = 0.5 * (3.0 * u * u - 1.0)
    vv = 0.5 * (3.0 * v * v - 1.0)
    return [None, u, v, u * v, uu, vv, u * vv]


def normal_kernel(region_rows, band_ref, ext_ref, exp_ref, mask_ref, par_ref, col_ref, out_ref, vert, design):
    bases = col_ref.shape[0]
    taps = col_ref.shape[1]
    rows, cols = exp_ref.shape
    wide = ext_ref.shape[1]
    fit = 3 * bases + 7
    half_cols = cols // 2
    blocks = half_cols // EDGE
    vert[...] = jnp.dot(band_ref[...], ext_ref[...], precision=HIGHEST, preferred_element_type=jnp.float32)
    low = lax.broadcasted_iota(jnp.int32, (1, EDGE), 1) < STAMP_W

    def pick(x):
        parts = []
        for m in range(cols // (2 * EDGE)):
            a = x[:, 2 * m * EDGE : (2 * m + 1) * EDGE]
            b = x[:, (2 * m + 1) * EDGE : (2 * m + 2) * EDGE]
            upper = par_ref[:, m * EDGE : (m + 1) * EDGE] > 0.5
            mine = jnp.where(low, a, b)
            other = pltpu.roll(jnp.where(low, b, a), STAMP_W, 1)
            parts.append(jnp.where(upper == low, other, mine))
        return jnp.concatenate(parts, axis=1)

    first = (lax.axis_index("stripe") * rows).astype(jnp.float32)
    v = jnp.broadcast_to(row_coords(first, rows, region_rows), (rows, half_cols))
    u_all = jnp.broadcast_to(col_coords(0.0, cols, cols), (8, cols))
    u = jnp.broadcast_to(pick(u_all)[0:1], (rows, half_cols))
    good = pick(mask_ref[...].astype(jnp.float32))

    def put(n, x):
        x = x * good
        for m in range(blocks):
            design[m, pl.ds(pl.multiple_of(n * rows, rows), rows), :] = x[:, m * EDGE : (m + 1) * EDGE]

    def each_basis(b, carry):
        x = vert[pl.ds(pl.multiple_of(b * rows, rows), rows), :]
        acc = jnp.zeros((rows, cols), jnp.float32)
        for j in range(taps):
            acc = acc + col_ref[b, j] * pltpu.roll(x, wide - (EDGE - HALF) - j, 1)[:, :cols]
        picked = pick(acc)
        put(3 * b, picked)
        put(3 * b + 1, picked * u)
        put(3 * b + 2, picked * v)
        return carry

    lax.fori_loop(0, bases, each_basis, 0)
    terms = background(u, v)
    terms[0] = jnp.ones_like(u)
    for m, term in enumerate(terms):
        put(3 * bases + m, term)
    put(fit, pick(exp_ref[...]))
    total = out_ref.shape[0]
    for n in range(fit + 1, total):
        put(n, jnp.zeros_like(u))
    acc = jnp.zeros((total, total), jnp.float32)
    for r in range(rows):
        x = [design[m, pl.ds(r, total, stride=rows), :] for m in range(blocks)]
        x = jnp.concatenate(x, axis=1).astype(jnp.bfloat16)
        acc = acc + lax.dot_general(x, x, (((1,), (1,)), ((), ())), preferred_element_type=jnp.float32)
    out_ref[...] = jnp.concatenate([acc, jnp.zeros((total, EDGE - total), jnp.float32)], axis=1)


def solve_kernel(count, fit, local_ref, out_ref, row_ref, send, held, send_sem, recv_sem):
    me = lax.axis_index("stripe")
    steps = []
    d = 1
    while d < count:
        steps.append(d)
        d *= 2
    partners = [me + d * (1 - 2 * ((me // d) % 2)) for d in steps]
    barrier = pltpu.get_barrier_semaphore()
    for partner in partners:
        pl.semaphore_signal(barrier, inc=1, device_id={"stripe": partner}, device_id_type=MESH)
    pl.semaphore_wait(barrier, len(partners))
    total = local_ref[...]
    for s, partner in enumerate(partners):
        source = local_ref
        if s:
            send[s] = total
            source = send.at[s]
        copy = pltpu.make_async_remote_copy(
            src_ref=source,
            dst_ref=held.at[s],
            send_sem=send_sem.at[s],
            recv_sem=recv_sem.at[s],
            device_id={"stripe": partner},
            device_id_type=MESH,
        )
        copy.start()
        copy.wait()
        total = total + held[s]
    a = total[:fit, :]
    sub = lax.broadcasted_iota(jnp.int32, a.shape, 0)
    lane = lax.broadcasted_iota(jnp.int32, a.shape, 1)
    for k in range(fit):
        row = a[k : k + 1, :]
        row = row / a[k : k + 1, k : k + 1]
        a = jnp.where(sub == k, row, a - a[:, k : k + 1] * row)
    answer = jnp.broadcast_to(a[:, fit : fit + 1], a.shape)
    out_ref[...] = jnp.zeros_like(out_ref)
    out_ref[:fit, :] = answer
    row_ref[...] = jnp.broadcast_to(
        jnp.sum(jnp.where(sub == lane, answer, 0.0), axis=0, keepdims=True), row_ref.shape
    )


def model_kernel(region_rows, bases, taps, coef_ref, ext_ref, exp_ref, mask_ref, rowf_ref, colf_ref, out_ref, band, wide_y, diff):
    rows, cols = out_ref.shape
    tall = exp_ref.shape[0]
    ext_rows, wide = ext_ref.shape
    first = (lax.axis_index("stripe") * rows - 1).astype(jnp.float32)
    v = row_coords(first, tall, region_rows)
    pad_b = rowf_ref.shape[0]
    mats = []
    for t in range(3):
        c = coef_ref[pl.ds(t, pad_b, stride=3), :]
        mats.append(
            lax.dot_general(
                colf_ref[...] * c,
                rowf_ref[...],
                (((0,), (0,)), ((), ())),
                precision=HIGHEST,
                preferred_element_type=jnp.float32,
            )
        )
    for j in range(taps):
        k0, k1, k2 = (jnp.broadcast_to(m[j : j + 1, :], (tall, EDGE)) for m in mats)
        main = k0 + v * k2 + (-(j - HALF) * 2.0 / cols) * k1
        main = pltpu.roll(main, 0, 1, stride=1, stride_axis=0)
        side = pltpu.roll(k1, ext_rows, 1, stride=1, stride_axis=0)
        band[j * tall : (j + 1) * tall, :] = main + side
    ext = ext_ref[...]
    u_wide = col_coords(-float(EDGE), wide, cols)
    both = jnp.concatenate([ext, ext * u_wide, jnp.zeros((EDGE - 2 * ext_rows, wide), jnp.float32)], axis=0)
    high = both.astype(jnp.bfloat16)
    rest = (both - high.astype(jnp.float32)).astype(jnp.bfloat16)
    weights = band[...]
    w_high = weights.astype(jnp.bfloat16)
    w_rest = (weights - w_high.astype(jnp.float32)).astype(jnp.bfloat16)
    dot = functools.partial(jnp.dot, preferred_element_type=jnp.float32)
    wide_y[...] = dot(w_high, high) + (dot(w_high, rest) + dot(w_rest, high))
    u = col_coords(0.0, cols, cols)
    q = [coef_ref[3 * bases + m : 3 * bases + m + 1, 0:1] for m in range(7)]
    terms = background(u, v)
    level = q[0] + q[1] * terms[1] + q[4] * terms[4]
    model = level + (q[2] * terms[2] + q[5] * terms[5]) + u * (q[3] * v + q[6] * terms[5])
    for j in range(taps):
        y = wide_y[j * tall : (j + 1) * tall, :]
        model = model + pltpu.roll(y, wide - (EDGE - HALF) - j, 1)[:, :cols]
    d = mask_ref[...] * (exp_ref[...] - model)
    diff[...] = d
    lane = lax.broadcasted_iota(jnp.int32, (rows, cols), 1)
    mid = diff[1 : rows + 1, :]
    left = jnp.where(lane == 0, 0.0, pltpu.roll(mid, 1, 1))
    right = jnp.where(lane == cols - 1, 0.0, pltpu.roll(mid, cols - 1, 1))
    around = diff[2 : rows + 2, :] + diff[0:rows, :] + right + left
    out_ref[...] = 4.0 * mid - around


def shards(template, exposure, cosmic_mask, stamp_blocks, row_filters, col_filters):
    rows, cols = exposure.shape[1:]
    bases, taps = row_filters.shape
    fit = 3 * bases + 7
    reach = HALF + 1
    stripes = lax.axis_size("stripe")
    region_rows = rows * stripes
    me_exp = lax.axis_index("exp")
    other = lax.ppermute(template, "exp", [(0, 1), (1, 0)])
    is_first = me_exp == 0
    full = jnp.concatenate([jnp.where(is_first, template, other), jnp.where(is_first, other, template)], axis=1)
    own_exp = exposure[0]
    own_mask = cosmic_mask[0].astype(jnp.float32)
    down = [(i, i + 1) for i in range(stripes - 1)]
    up = [(i + 1, i) for i in range(stripes - 1)]
    above = lax.ppermute(jnp.concatenate([full[rows - reach :], own_exp[rows - 1 :], own_mask[rows - 1 :]]), "stripe", down)
    below = lax.ppermute(jnp.concatenate([full[:reach], own_exp[:1], own_mask[:1]]), "stripe", up)
    ext_rows = round_up(rows + 2 * reach, 8)
    ext = jnp.concatenate([above[:reach], full, below[:reach]], axis=0)
    ext = jnp.pad(ext, ((0, ext_rows - ext.shape[0]), (EDGE, EDGE)))
    wide = ext.shape[1]
    tall = round_up(rows + 2, 8)
    spare = jnp.zeros((tall - rows - 2, cols), jnp.float32)
    exp_tall = jnp.concatenate([above[reach : reach + 1], own_exp, below[reach : reach + 1], spare])
    mask_tall = jnp.concatenate([above[reach + 1 :], own_mask, below[reach + 1 :], spare])
    tap = jnp.arange(ext_rows)[None, :] - jnp.arange(rows)[:, None] - 1
    band = jnp.zeros((bases, rows, ext_rows), jnp.float32)
    for i in range(taps):
        band = band + jnp.where((tap == i)[None], row_filters[:, i][:, None, None], 0.0)
    band = band.reshape(bases * rows, ext_rows)
    parity = jnp.repeat((stamp_blocks % 2).astype(jnp.float32), STAMP_W, axis=1)
    pad_b = round_up(bases, 8)
    row_pad = jnp.pad(row_filters, ((0, pad_b - bases), (0, EDGE - taps)))
    col_pad = jnp.pad(col_filters, ((0, pad_b - bases), (0, EDGE - taps)))
    total = round_up(fit + 1, 8)
    vmem = pl.BlockSpec(memory_space=pltpu.VMEM)
    smem = pl.BlockSpec(memory_space=pltpu.SMEM)
    f32 = jnp.float32
    normal = pl.pallas_call(
        functools.partial(normal_kernel, float(region_rows)),
        out_shape=jax.ShapeDtypeStruct((total, EDGE), f32),
        in_specs=[vmem] * 5 + [smem],
        out_specs=vmem,
        scratch_shapes=[pltpu.VMEM((bases * rows, wide), f32), pltpu.VMEM((cols // (2 * EDGE), total * rows, EDGE), f32)],
        name="normal",
    )(band, ext, own_exp, cosmic_mask[0], parity, col_filters)
    hops = max(1, (stripes - 1).bit_length())
    coef, coef_row = pl.pallas_call(
        functools.partial(solve_kernel, stripes, fit),
        out_shape=(jax.ShapeDtypeStruct((total, EDGE), f32), jax.ShapeDtypeStruct((8, EDGE), f32)),
        in_specs=[vmem],
        out_specs=(vmem, vmem),
        scratch_shapes=[
            pltpu.VMEM((hops, total, EDGE), f32),
            pltpu.VMEM((hops, total, EDGE), f32),
            pltpu.SemaphoreType.DMA((hops,)),
            pltpu.SemaphoreType.DMA((hops,)),
        ],
        compiler_params=pltpu.CompilerParams(collective_id=0, has_side_effects=True),
        name="solve",
    )(normal)
    filtered = pl.pallas_call(
        functools.partial(model_kernel, float(region_rows), bases, taps),
        out_shape=jax.ShapeDtypeStruct((rows, cols), f32),
        in_specs=[vmem] * 6,
        out_specs=vmem,
        scratch_shapes=[
            pltpu.VMEM((taps * tall, EDGE), f32),
            pltpu.VMEM((taps * tall, wide), f32),
            pltpu.VMEM((tall, cols), f32),
        ],
        name="model",
    )(coef, ext, exp_tall, mask_tall, row_pad, col_pad)
    return (filtered[None], coef_row[:1, :fit])


def solution(mesh):
    placed = (
        P(("groups", "stripe"), "exp"),
        P(("groups", "exp"), "stripe", None),
        P(("groups", "exp"), "stripe", None),
        P(("groups", "stripe"), None),
        P(),
        P(),
    )
    return jax.shard_map(
        shards,
        mesh=mesh,
        in_specs=placed,
        out_specs=(P(("groups", "exp"), "stripe", None), P(("groups", "exp"), None)),
        check_vma=False,
    )
```

profile of v0, /device:TPU:0, one launch (start us, length us, event | category | flops | bytes accessed | tf_op | source)
XLA Modules:
  0.0 70.5 jit_solution(921996981298710876)
XLA Ops:
  0.6 0.6 collective-permute-start
  1.3 0.6 copy-done
  1.9 0.5 slice_reduce_fusion.18
  2.4 0.1 broadcast_in_dim.405
  2.5 0.1 broadcast_in_dim.406
  2.6 0.1 broadcast_in_dim.412
  2.6 0.1 broadcast_in_dim.413
  2.7 0.1 broadcast_in_dim.418
  2.8 0.1 broadcast_in_dim.419
  2.9 0.1 broadcast_in_dim.424
  2.9 0.1 broadcast_in_dim.425
  3.0 0.1 broadcast_in_dim.430
  3.1 0.1 broadcast_in_dim.431
  3.2 0.1 broadcast_in_dim.436
  3.3 0.1 broadcast_in_dim.437
  3.3 0.1 broadcast_in_dim.442
  3.4 0.1 broadcast_in_dim.443
  3.6 0.1 broadcast_in_dim.449
  3.7 0.1 broadcast_in_dim.455
  3.9 0.1 broadcast_in_dim.461
  4.0 0.1 broadcast_in_dim.466
  4.1 0.1 broadcast_in_dim.467
  4.2 0.1 broadcast_in_dim.473
  4.4 0.1 broadcast_in_dim.479
  4.5 0.1 broadcast_in_dim.485
  4.7 0.1 broadcast_in_dim.491
  4.8 0.1 broadcast_in_dim.497
  5.0 0.1 broadcast_in_dim.503
  5.1 0.1 broadcast_in_dim.509
  5.3 0.1 broadcast_in_dim.515
  5.5 0.9 %slice_bitcast_fusion.1 = (f32[1,2048]{1,0:T(1,128)S(1)}, f32[1,2048]{1,0:T(1,128)S(1)}) fusion(f32[1,16,2048]{2,1,0:T(8,128)} %param.7), kind=kLoop, calls=%fused_computation.43 | loop fusion | bytes 32768 | tf_op jit(solution)/shard_map/slice | solution.py:210
  6.4 0.1 broadcast_in_dim.517
  6.5 0.7 broadcast_in_dim.518.par_ref
  7.2 0.6 pad.12.rowf_ref
  7.8 0.1 copy-done.4
  7.9 0.6 pad.13.colf_ref
  8.5 0.1 pad.21.clone
  8.7 4.4 %collective-permute-start.1 = (f32[12,2048]{1,0:T(8,128)S(1)}, f32[12,2048]{1,0:T(8,128)S(1)}, u32[]{:S(2)}, u32[]{:S(2)}) collective-permute-start(f32[12,2048]{1,0:T(8,128)S(1)} %pad_maximum_fusion), channel_id=1, source_target_pairs={{0,2},{2,4},{4,6},{6,8},{8,10},{10,12},{12,14},{1,3},{3,5},{5,7},{... | collective-permute-start | bytes 294920 | tf_op jit(solution)/shard_map/ppermute | solution.py:210
  13.1 1.3 %collective-permute-start.2 = (f32[12,2048]{1,0:T(8,128)S(1)}, f32[12,2048]{1,0:T(8,128)S(1)}, u32[]{:S(2)}, u32[]{:S(2)}) collective-permute-start(f32[12,2048]{1,0:T(8,128)S(1)} %fusion.8), channel_id=1, source_target_pairs={{2,0},{4,2},{6,4},{8,6},{10,8},{12,10},{14,12},{3,1},{5,3},{7,5},{... | collective-permute-start | bytes 294920 | tf_op jit(solution)/shard_map/ppermute | solution.py:211
  14.4 1.5 %select_add_fusion.band_ref = f32[304,40]{1,0:T(8,128)} fusion(f32[304]{0:T(512)S(1)} %broadcast_in_dim.515, f32[304]{0:T(512)S(1)} %broadcast_in_dim.509, f32[304]{0:T(512)S(1)} %broadcast_in_dim.503, f32[304]{0:T(512)S(1)} %broadcast_in_dim.497, f32[304]{0:T(512)S(1)} %broadcast_in_dim.491, f32[304]{0:T(512)S(1)} %broadcast_in_dim.485, ...), kind=kLoop, calls=%fused_computation.14 | loop fusion | flops 449920 | bytes 83904 | tf_op jit(solution)/shard_map/add | solution.py:223
  16.0 0.5 collective-permute-done.1
  16.5 4.2 %collective-permute-done.2 = f32[12,2048]{1,0:T(8,128)S(1)} collective-permute-done((f32[12,2048]{1,0:T(8,128)S(1)}, f32[12,2048]{1,0:T(8,128)S(1)}, u32[]{:S(2)}, u32[]{:S(2)}) %collective-permute-start.2) | collective-permute-done | bytes 98336 | tf_op jit(solution)/shard_map/ppermute | solution.py:211
  20.6 0.8 %select_maximum_fusion.ext_ref = f32[40,2304]{1,0:T(8,128)} fusion(f32[10,2048]{1,0:T(8,128)S(1)} %bitcast.54, f32[10,2048]{1,0:T(8,128)S(1)} %bitcast.53, f32[16,1024]{1,0:T(8,128)S(1)} %get-tuple-element.34, f32[16,1024]{1,0:T(8,128)S(1)} %get-tuple-element.33), kind=kLoop, calls=%fused_computation.2 | loop fusion | flops 1474560 | bytes 663552 | tf_op jit(solution)/shard_map/concatenate | solution.py:213
  21.4 22.3 %normal.1.local_ref = f32[72,128]{1,0:T(8,128)} custom-call(f32[304,40]{1,0:T(8,128)} %select_add_fusion.band_ref, f32[40,2304]{1,0:T(8,128)} %select_maximum_fusion.ext_ref, f32[16,2048]{1,0:T(8,128)} %bitcast.50, s32[16,2048]{1,0:T(8,128)} %bitcast.52, f32[1,1024]{1,0:T(1,128)} %broadcast_in_dim.518.par_ref, f32[19,19]{1,0:T(8,128)} %col_ref.1), custom_call_target="tpu_custom_call" | custom-call | tf_op jit(solution)/shard_map/normal/pallas_call | solution.py:233
  43.7 19.9 %solve.1 = (f32[72,128]{1,0:T(8,128)}, f32[8,128]{1,0:T(8,128)}) custom-call(f32[72,128]{1,0:T(8,128)} %normal.1.local_ref), custom_call_target="tpu_custom_call" | custom-call | tf_op jit(solution)/shard_map/solve/pallas_call | solution.py:242
  63.7 1.2 %slice.135 = f32[1,64]{1,0:T(1,128)} slice(f32[8,128]{1,0:T(8,128)} %get-tuple-element.5), slice={[0:1], [0:64]} | slice | bytes 512 | tf_op jit(solution)/shard_map/slice | solution.py:268
  64.9 0.8 %maximum_maximum_fusion.1 = (f32[24,2048]{1,0:T(8,128)}, f32[24,2048]{1,0:T(8,128)}) fusion(f32[1,2048]{1,0:T(1,128)S(1)} %get-tuple-element.27, f32[16,2048]{1,0:T(8,128)S(1)} %bitcast_convert_fusion, f32[1,2048]{1,0:T(1,128)S(1)} %get-tuple-element.25, f32[24]{0:T(128)S(1)} %pad.21.clone, f32[1,2048]{1,0:T(1,128)S(1)} %get-tuple-element.28, ...), kind=kLoop, calls=%fused_computation.13 | loop fusion | flops 294912 | bytes 688224 | tf_op jit(solution)/shard_map/concatenate | solution.py:219
  65.8 4.8 %model.1 = f32[16,2048]{1,0:T(8,128)} custom-call(f32[72,128]{1,0:T(8,128)} %get-tuple-element.4.coef_ref, f32[40,2304]{1,0:T(8,128)} %select_maximum_fusion.ext_ref, f32[24,2048]{1,0:T(8,128)} %get-tuple-element.36.exp_ref, f32[24,2048]{1,0:T(8,128)} %get-tuple-element.35.mask_ref, f32[24,128]{1,0:T(8,128)} %pad.12.rowf_ref, f32[24,128]{1,0:T(8,128)} %pad.13.colf_ref), custom_call_target="tpu_custom_call" | custom-call | tf_op jit(solution)/shard_map/model/pallas_call | solution.py:256
  (42 shorter events, 1.1 us)
Async XLA Ops:
  0.6 7.9 %collective-permute-start = (f32[16,1024]{1,0:T(8,128)}, f32[16,1024]{1,0:T(8,128)S(1)}, u32[]{:S(2)}, u32[]{:S(2)}) collective-permute-start(f32[16,1024]{1,0:T(8,128)} %param.6), channel_id=1, source_target_pairs={{0,1},{1,0},{2,3},{3,2},{4,5},{5,4},{6,7},{7,6},{8,9},{9,8},{10,11... | collective-permute-start | bytes 196616 | tf_op jit(solution)/shard_map/ppermute | solution.py:203
  1.2 0.7 %copy-start = (f32[19,19]{1,0:T(8,128)S(1)}, f32[19,19]{1,0:T(8,128)}, u32[]{:S(2)}) copy-start(f32[19,19]{1,0:T(8,128)} %param.10) | copy-start | bytes 4336
  4.0 1.4 %copy-start.2 = (s32[1,16,2048]{2,1,0:T(8,128)S(1)}, s32[1,16,2048]{2,1,0:T(8,128)}, u32[]{:S(2)}) copy-start(s32[1,16,2048]{2,1,0:T(8,128)} %param.8) | copy-start | bytes 393220
  5.4 1.0 %copy-start.5 = (s32[1,16]{1,0:T(1,128)S(1)}, s32[1,16]{1,0:T(1,128)}, u32[]{:S(2)}) copy-start(s32[1,16]{1,0:T(1,128)} %param.9) | copy-start | bytes 196
  5.5 3.1 %copy-start.3 = (f32[16,1024]{1,0:T(8,128)S(1)}, f32[16,1024]{1,0:T(8,128)}, u32[]{:S(2)}) copy-start(f32[16,1024]{1,0:T(8,128)} %param.6) | copy-start | bytes 196612
  7.2 0.7 %copy-start.4 = (f32[19,19]{1,0:T(8,128)S(1)}, f32[19,19]{1,0:T(8,128)}, u32[]{:S(2)}) copy-start(f32[19,19]{1,0:T(8,128)} %col_ref.1) | copy-start | bytes 4336
  8.7 7.8 %collective-permute-start.1 = (f32[12,2048]{1,0:T(8,128)S(1)}, f32[12,2048]{1,0:T(8,128)S(1)}, u32[]{:S(2)}, u32[]{:S(2)}) collective-permute-start(f32[12,2048]{1,0:T(8,128)S(1)} %pad_maximum_fusion), channel_id=1, source_target_pairs={{0,2},{2,4},{4,6},{6,8},{8,10},{10,12},{12,14},{1,3},{3,5},{5,7},{... | collective-permute-start | bytes 294920 | tf_op jit(solution)/shard_map/ppermute | solution.py:210
  13.1 7.5 %collective-permute-start.2 = (f32[12,2048]{1,0:T(8,128)S(1)}, f32[12,2048]{1,0:T(8,128)S(1)}, u32[]{:S(2)}, u32[]{:S(2)}) collective-permute-start(f32[12,2048]{1,0:T(8,128)S(1)} %fusion.8), channel_id=1, source_target_pairs={{2,0},{4,2},{6,4},{8,6},{10,8},{12,10},{14,12},{3,1},{5,3},{7,5},{... | collective-permute-start | bytes 294920 | tf_op jit(solution)/shard_map/ppermute | solution.py:211
  21.4 43.5 %copy-start.1 = (f32[1,16,2048]{2,1,0:T(8,128)S(1)}, f32[1,16,2048]{2,1,0:T(8,128)}, u32[]{:S(2)}) copy-start(f32[1,16,2048]{2,1,0:T(8,128)} %param.7) | copy-start | bytes 393220
where the time goes:
time: 71 us; the launch traced here: 70.5 us
  Pallas kernels  47 us (66%)
  local copies, waits for them, and re-layouts  8.33 us (12%)
  starting transfers between devices  6.26 us (9%)
  waiting for transfers between devices  4.64 us (7%)
  other arithmetic  3.38 us (5%)
  between operations  0.86 us (1%)
    pallas_call x1, Pallas kernels, shards(): pl.pallas_call(functools.partial(normal_kernel, float(region_rows)), out_...  22.3 us
    pallas_call x1, Pallas kernels, shards(): pl.pallas_call(functools.partial(solve_kernel, stripes, fit), out_shape=(...  19.9 us
    pallas_call x1, Pallas kernels, shards(): pl.pallas_call(functools.partial(model_kernel, float(region_rows), bases,...  4.75 us
    ppermute x1, starting transfers between devices, shards(): lax.ppermute(jnp.concatenate([full[rows - reach:], own_exp[rows - 1:], ow...  4.41 us
    ppermute x1, waiting for transfers between devices, shards(): lax.ppermute(jnp.concatenate([full[:reach], own_exp[:1], own_mask[:1]]),...  4.16 us
    broadcast_in_dim x38, local copies, waits for them, and re-layouts, shards(): jnp.where((tap == i)[None], row_filters[:, i][:, None, None], 0.0)  2.92 us
    add x1, other arithmetic, shards(): band + jnp.where((tap == i)[None], row_filters[:, i][:, None, None], 0.0)  1.54 us
  transfers between devices with their start and end apart: 3, of which 2 were waited for; matrix products, arithmetic and copies ran while one was open for 11% of the time, Pallas kernels for 0%

commit v1 on v0

--- a/solution.py
+++ b/solution.py
@@ -34,26 +34,56 @@
     return [None, u, v, u * v, uu, vv, u * vv]
 
 
-def normal_kernel(region_rows, band_ref, ext_ref, exp_ref, mask_ref, par_ref, col_ref, out_ref, vert, design):
-    bases = col_ref.shape[0]
-    taps = col_ref.shape[1]
+def split(x):
+    high = x.astype(jnp.bfloat16)
+    return high, (x - high.astype(jnp.float32)).astype(jnp.bfloat16)
+
+
+def shifted_rows(row, count, start):
+    return pltpu.roll(jnp.broadcast_to(row, (count, EDGE)), start, 1, stride=1, stride_axis=0)
+
+
+def normal_kernel(region_rows, ext_ref, exp_ref, mask_ref, blk_ref, rowf_ref, colf_ref, out_ref, bandw, vert, design):
+    bases, taps = rowf_ref.shape
     rows, cols = exp_ref.shape
-    wide = ext_ref.shape[1]
+    ext_rows = ext_ref.shape[0]
     fit = 3 * bases + 7
+    total = out_ref.shape[0]
     half_cols = cols // 2
     blocks = half_cols // EDGE
-    vert[...] = jnp.dot(band_ref[...], ext_ref[...], precision=HIGHEST, preferred_element_type=jnp.float32)
+    stamps = 2 * blocks
     low = lax.broadcasted_iota(jnp.int32, (1, EDGE), 1) < STAMP_W
+    parity = [blk_ref[0, s] % 2 == 1 for s in range(stamps)]
+    lanes = jnp.zeros((1, EDGE - taps), jnp.float32)
+
+    windows = []
+    for s in range(stamps):
+        part = ext_ref[:, s * EDGE : (s + 3) * EDGE]
+        early = pltpu.roll(part, 2 * EDGE + HALF, 1)[:, :EDGE]
+        late = pltpu.roll(part, 2 * EDGE + HALF - STAMP_W, 1)[:, :EDGE]
+        windows.append(jnp.where(parity[s], late, early))
+    window = jnp.concatenate(windows, axis=1)
+    w_high, w_rest = split(window)
+    gap = jnp.zeros((EDGE - 2 * ext_rows, window.shape[1]), jnp.bfloat16)
+    gap2 = jnp.zeros((EDGE - ext_rows, window.shape[1]), jnp.bfloat16)
+    stacked = jnp.concatenate([w_high, w_rest, gap, w_high, gap2], axis=0)
+    start = ext_rows // 2 - rows // 2 - HALF
+    for b in range(bases):
+        row = jnp.concatenate([rowf_ref[b : b + 1, :], lanes], axis=1)
+        high = row.astype(jnp.bfloat16).astype(jnp.float32)
+        twice = shifted_rows(high, rows, start) + shifted_rows(high, rows, start + ext_rows)
+        rest = shifted_rows(row - high, rows, start)
+        bandw[b * rows : (b + 1) * rows, :] = jnp.concatenate([twice, rest], axis=1)
+    vert[...] = jnp.dot(bandw[...].astype(jnp.bfloat16), stacked, preferred_element_type=jnp.float32)
 
     def pick(x):
         parts = []
-        for m in range(cols // (2 * EDGE)):
+        for m in range(blocks):
             a = x[:, 2 * m * EDGE : (2 * m + 1) * EDGE]
             b = x[:, (2 * m + 1) * EDGE : (2 * m + 2) * EDGE]
-            upper = par_ref[:, m * EDGE : (m + 1) * EDGE] > 0.5
-            mine = jnp.where(low, a, b)
-            other = pltpu.roll(jnp.where(low, b, a), STAMP_W, 1)
-            parts.append(jnp.where(upper == low, other, mine))
+            a = jnp.where(parity[2 * m], pltpu.roll(a, STAMP_W, 1), a)
+            b = jnp.where(parity[2 * m + 1], b, pltpu.roll(b, STAMP_W, 1))
+            parts.append(jnp.where(low, a, b))
         return jnp.concatenate(parts, axis=1)
 
     first = (lax.axis_index("stripe") * rows).astype(jnp.float32)
@@ -65,26 +95,39 @@
     def put(n, x):
         x = x * good
         for m in range(blocks):
-            design[m, pl.ds(pl.multiple_of(n * rows, rows), rows), :] = x[:, m * EDGE : (m + 1) * EDGE]
-
-    def each_basis(b, carry):
-        x = vert[pl.ds(pl.multiple_of(b * rows, rows), rows), :]
-        acc = jnp.zeros((rows, cols), jnp.float32)
-        for j in range(taps):
-            acc = acc + col_ref[b, j] * pltpu.roll(x, wide - (EDGE - HALF) - j, 1)[:, :cols]
-        picked = pick(acc)
+            design[m, n * rows : (n + 1) * rows, :] = x[:, m * EDGE : (m + 1) * EDGE]
+
+    for b in range(bases):
+        x = vert[b * rows : (b + 1) * rows, :]
+        x = jnp.concatenate([x[:, s * EDGE : (s + 1) * EDGE] for s in range(stamps)], axis=0)
+        x_high, x_rest = split(x)
+        row = jnp.concatenate([colf_ref[b : b + 1, :], lanes], axis=1)
+        t_high, t_rest = split(shifted_rows(row, STAMP_W, 0))
+        upper = jnp.concatenate([t_high, t_high], axis=1)
+        lower = jnp.concatenate([t_rest, jnp.zeros_like(t_rest)], axis=1)
+        y = lax.dot_general(
+            jnp.concatenate([x_high, x_rest], axis=1),
+            jnp.concatenate([upper, lower], axis=0),
+            (((1,), (1,)), ((), ())),
+            preferred_element_type=jnp.float32,
+        )
+        y = y + pltpu.roll(y, STAMP_W, 1)
+        picked = jnp.concatenate(
+            [
+                jnp.where(low, y[2 * m * rows : (2 * m + 1) * rows], y[(2 * m + 1) * rows : (2 * m + 2) * rows])
+                for m in range(blocks)
+            ],
+            axis=1,
+        )
         put(3 * b, picked)
         put(3 * b + 1, picked * u)
         put(3 * b + 2, picked * v)
-        return carry
-
-    lax.fori_loop(0, bases, each_basis, 0)
+
     terms = background(u, v)
     terms[0] = jnp.ones_like(u)
     for m, term in enumerate(terms):
         put(3 * bases + m, term)
     put(fit, pick(exp_ref[...]))
-    total = out_ref.shape[0]
     for n in range(fit + 1, total):
         put(n, jnp.zeros_like(u))
     acc = jnp.zeros((total, total), jnp.float32)
@@ -95,7 +138,7 @@
     out_ref[...] = jnp.concatenate([acc, jnp.zeros((total, EDGE - total), jnp.float32)], axis=1)
 
 
-def solve_kernel(count, fit, local_ref, out_ref, row_ref, send, held, send_sem, recv_sem):
+def solve_kernel(count, fit, local_ref, out_ref, send, held, send_sem, recv_sem):
     me = lax.axis_index("stripe")
     steps = []
     d = 1
@@ -126,33 +169,36 @@
         total = total + held[s]
     a = total[:fit, :]
     sub = lax.broadcasted_iota(jnp.int32, a.shape, 0)
-    lane = lax.broadcasted_iota(jnp.int32, a.shape, 1)
     for k in range(fit):
         row = a[k : k + 1, :]
-        row = row / a[k : k + 1, k : k + 1]
+        row = row * pl.reciprocal(jnp.broadcast_to(a[k : k + 1, k : k + 1], row.shape))
         a = jnp.where(sub == k, row, a - a[:, k : k + 1] * row)
     answer = jnp.broadcast_to(a[:, fit : fit + 1], a.shape)
     out_ref[...] = jnp.zeros_like(out_ref)
     out_ref[:fit, :] = answer
-    row_ref[...] = jnp.broadcast_to(
-        jnp.sum(jnp.where(sub == lane, answer, 0.0), axis=0, keepdims=True), row_ref.shape
-    )
-
-
-def model_kernel(region_rows, bases, taps, coef_ref, ext_ref, exp_ref, mask_ref, rowf_ref, colf_ref, out_ref, band, wide_y, diff):
+
+
+def model_kernel(region_rows, coef_ref, ext_ref, exp_ref, mask_ref, rowf_ref, colf_ref, out_ref, row_ref, band, wide_y, diff):
     rows, cols = out_ref.shape
+    bases, taps = rowf_ref.shape
+    fit = 3 * bases + 7
     tall = exp_ref.shape[0]
+    answer = coef_ref[:fit, :fit]
+    same = lax.broadcasted_iota(jnp.int32, (fit, fit), 0) == lax.broadcasted_iota(jnp.int32, (fit, fit), 1)
+    row_ref[...] = jnp.sum(jnp.where(same, answer, 0.0), axis=0, keepdims=True)
     ext_rows, wide = ext_ref.shape
     first = (lax.axis_index("stripe") * rows - 1).astype(jnp.float32)
     v = row_coords(first, tall, region_rows)
-    pad_b = rowf_ref.shape[0]
+    rowf = jnp.concatenate([rowf_ref[...], jnp.zeros((bases, EDGE - taps), jnp.float32)], axis=1)
+    colf = jnp.concatenate([colf_ref[...], jnp.zeros((bases, EDGE - taps), jnp.float32)], axis=1)
+    start = ext_rows // 2 - rows // 2 - HALF - 1
     mats = []
     for t in range(3):
-        c = coef_ref[pl.ds(t, pad_b, stride=3), :]
+        c = coef_ref[pl.ds(t, bases, stride=3), :]
         mats.append(
             lax.dot_general(
-                colf_ref[...] * c,
-                rowf_ref[...],
+                colf * c,
+                rowf,
                 (((0,), (0,)), ((), ())),
                 precision=HIGHEST,
                 preferred_element_type=jnp.float32,
@@ -161,17 +207,14 @@
     for j in range(taps):
         k0, k1, k2 = (jnp.broadcast_to(m[j : j + 1, :], (tall, EDGE)) for m in mats)
         main = k0 + v * k2 + (-(j - HALF) * 2.0 / cols) * k1
-        main = pltpu.roll(main, 0, 1, stride=1, stride_axis=0)
-        side = pltpu.roll(k1, ext_rows, 1, stride=1, stride_axis=0)
+        main = shifted_rows(main, tall, start)
+        side = shifted_rows(k1, tall, start + ext_rows)
         band[j * tall : (j + 1) * tall, :] = main + side
     ext = ext_ref[...]
     u_wide = col_coords(-float(EDGE), wide, cols)
     both = jnp.concatenate([ext, ext * u_wide, jnp.zeros((EDGE - 2 * ext_rows, wide), jnp.float32)], axis=0)
-    high = both.astype(jnp.bfloat16)
-    rest = (both - high.astype(jnp.float32)).astype(jnp.bfloat16)
-    weights = band[...]
-    w_high = weights.astype(jnp.bfloat16)
-    w_rest = (weights - w_high.astype(jnp.float32)).astype(jnp.bfloat16)
+    high, rest = split(both)
+    w_high, w_rest = split(band[...])
     dot = functools.partial(jnp.dot, preferred_element_type=jnp.float32)
     wide_y[...] = dot(w_high, high) + (dot(w_high, rest) + dot(w_rest, high))
     u = col_coords(0.0, cols, cols)
@@ -209,23 +252,15 @@
     up = [(i + 1, i) for i in range(stripes - 1)]
     above = lax.ppermute(jnp.concatenate([full[rows - reach :], own_exp[rows - 1 :], own_mask[rows - 1 :]]), "stripe", down)
     below = lax.ppermute(jnp.concatenate([full[:reach], own_exp[:1], own_mask[:1]]), "stripe", up)
-    ext_rows = round_up(rows + 2 * reach, 8)
+    side = round_up(reach, 16)
+    ext_rows = rows + 2 * side
     ext = jnp.concatenate([above[:reach], full, below[:reach]], axis=0)
-    ext = jnp.pad(ext, ((0, ext_rows - ext.shape[0]), (EDGE, EDGE)))
+    ext = jnp.pad(ext, ((side - reach, side - reach), (EDGE, EDGE)))
     wide = ext.shape[1]
     tall = round_up(rows + 2, 8)
     spare = jnp.zeros((tall - rows - 2, cols), jnp.float32)
     exp_tall = jnp.concatenate([above[reach : reach + 1], own_exp, below[reach : reach + 1], spare])
     mask_tall = jnp.concatenate([above[reach + 1 :], own_mask, below[reach + 1 :], spare])
-    tap = jnp.arange(ext_rows)[None, :] - jnp.arange(rows)[:, None] - 1
-    band = jnp.zeros((bases, rows, ext_rows), jnp.float32)
-    for i in range(taps):
-        band = band + jnp.where((tap == i)[None], row_filters[:, i][:, None, None], 0.0)
-    band = band.reshape(bases * rows, ext_rows)
-    parity = jnp.repeat((stamp_blocks % 2).astype(jnp.float32), STAMP_W, axis=1)
-    pad_b = round_up(bases, 8)
-    row_pad = jnp.pad(row_filters, ((0, pad_b - bases), (0, EDGE - taps)))
-    col_pad = jnp.pad(col_filters, ((0, pad_b - bases), (0, EDGE - taps)))
     total = round_up(fit + 1, 8)
     vmem = pl.BlockSpec(memory_space=pltpu.VMEM)
     smem = pl.BlockSpec(memory_space=pltpu.SMEM)
@@ -233,17 +268,21 @@
     normal = pl.pallas_call(
         functools.partial(normal_kernel, float(region_rows)),
         out_shape=jax.ShapeDtypeStruct((total, EDGE), f32),
-        in_specs=[vmem] * 5 + [smem],
+        in_specs=[vmem] * 3 + [smem] + [vmem] * 2,
         out_specs=vmem,
-        scratch_shapes=[pltpu.VMEM((bases * rows, wide), f32), pltpu.VMEM((cols // (2 * EDGE), total * rows, EDGE), f32)],
+        scratch_shapes=[
+            pltpu.VMEM((bases * rows, 2 * EDGE), f32),
+            pltpu.VMEM((bases * rows, cols), f32),
+            pltpu.VMEM((cols // (2 * EDGE), total * rows, EDGE), f32),
+        ],
         name="normal",
-    )(band, ext, own_exp, cosmic_mask[0], parity, col_filters)
+    )(ext, own_exp, cosmic_mask[0], stamp_blocks, row_filters, col_filters)
     hops = max(1, (stripes - 1).bit_length())
-    coef, coef_row = pl.pallas_call(
+    coef = pl.pallas_call(
         functools.partial(solve_kernel, stripes, fit),
-        out_shape=(jax.ShapeDtypeStruct((total, EDGE), f32), jax.ShapeDtypeStruct((8, EDGE), f32)),
+        out_shape=jax.ShapeDtypeStruct((total, EDGE), f32),
         in_specs=[vmem],
-        out_specs=(vmem, vmem),
+        out_specs=vmem,
         scratch_shapes=[
             pltpu.VMEM((hops, total, EDGE), f32),
             pltpu.VMEM((hops, total, EDGE), f32),
@@ -253,19 +292,19 @@
         compiler_params=pltpu.CompilerParams(collective_id=0, has_side_effects=True),
         name="solve",
     )(normal)
-    filtered = pl.pallas_call(
-        functools.partial(model_kernel, float(region_rows), bases, taps),
-        out_shape=jax.ShapeDtypeStruct((rows, cols), f32),
+    filtered, coef_row = pl.pallas_call(
+        functools.partial(model_kernel, float(region_rows)),
+        out_shape=(jax.ShapeDtypeStruct((rows, cols), f32), jax.ShapeDtypeStruct((1, fit), f32)),
         in_specs=[vmem] * 6,
-        out_specs=vmem,
+        out_specs=(vmem, vmem),
         scratch_shapes=[
             pltpu.VMEM((taps * tall, EDGE), f32),
             pltpu.VMEM((taps * tall, wide), f32),
             pltpu.VMEM((tall, cols), f32),
         ],
         name="model",
-    )(coef, ext, exp_tall, mask_tall, row_pad, col_pad)
-    return (filtered[None], coef_row[:1, :fit])
+    )(coef, ext, exp_tall, mask_tall, row_filters, col_filters)
+    return (filtered[None], coef_row)
 
 
 def solution(mesh):

time: 71 us -> 48.3 us (0.68)
  Pallas kernels: 47 us -> 31.2 us
  local copies, waits for them, and re-layouts: 8.33 us -> 1.02 us
  waiting for transfers between devices: 4.64 us -> 6.12 us
    pallas_call x1, Pallas kernels: 22.3 us -> 6.42 us  [shards(): pl.pallas_call(functools.partial(normal_kernel, float(region_rows)), out_...]
    broadcast_in_dim x40 -> x0, local copies, waits for them, and re-layouts: 3.66 us -> none  [the longest x38 2.92 us: shards(): jnp.where((tap == i)[None], row_filters[:, i][:, None, None], 0.0)]
    slice x2 -> x0, local copies, waits for them, and re-layouts: 1.69 us -> none  [the longest x1 1.19 us: shards(): return (filtered[None], coef_row[:1, :fit])]
    add x1 -> x0, other arithmetic: 1.54 us -> none  [shards(): band + jnp.where((tap == i)[None], row_filters[:, i][:, None, None], 0.0)]
    ppermute x1, waiting for transfers between devices: 0.49 us -> 1.96 us  [shards(): lax.ppermute(jnp.concatenate([full[rows - reach:], own_exp[rows - 1:], ow...]
    pad x2 -> x0, local copies, waits for them, and re-layouts: 1.2 us -> none  [the longest x1 0.6 us: shards(): col_pad = jnp.pad(col_filters, ((0, pad_b - bases), (0, EDGE - taps)))]
    convert_element_type x1, other arithmetic: 0.02 us -> 0.95 us  [shards(): own_mask = cosmic_mask[0].astype(jnp.float32)]
    unnamed x12 -> x4, local copies, waits for them, and re-layouts: 0.74 us -> 0.01 us
  transfers between devices with their start and end apart: 3 -> 3, of which waited for: 2 -> 2; matrix products, arithmetic and copies ran while one was open for 11% -> 4% of each run, Pallas kernels for 0% -> 0%
where the time goes in v1:
time: 48.3 us; the launch traced here: 48 us
  Pallas kernels  31.2 us (65%)
  starting transfers between devices  6.26 us (13%)
  waiting for transfers between devices  6.12 us (13%)
  other arithmetic  2.7 us (6%)
  local copies, waits for them, and re-layouts  1.02 us (2%)
  between operations  0.76 us (2%)
    pallas_call x1, Pallas kernels, shards(): pl.pallas_call(functools.partial(solve_kernel, stripes, fit), out_shape=j...  20 us
    pallas_call x1, Pallas kernels, shards(): pl.pallas_call(functools.partial(normal_kernel, float(region_rows)), out_...  6.42 us
    pallas_call x1, Pallas kernels, shards(): pl.pallas_call(functools.partial(model_kernel, float(region_rows)), out_s...  4.78 us
    ppermute x1, starting transfers between devices, shards(): lax.ppermute(jnp.concatenate([full[rows - reach:], own_exp[rows - 1:], ow...  4.41 us
    ppermute x1, waiting for transfers between devices, shards(): lax.ppermute(jnp.concatenate([full[:reach], own_exp[:1], own_mask[:1]]),...  4.16 us
    ppermute x1, waiting for transfers between devices, shards(): lax.ppermute(jnp.concatenate([full[rows - reach:], own_exp[rows - 1:], ow...  1.96 us
    ppermute x1, starting transfers between devices, shards(): lax.ppermute(jnp.concatenate([full[:reach], own_exp[:1], own_mask[:1]]),...  1.29 us
  transfers between devices with their start and end apart: 3, of which 2 were waited for; matrix products, arithmetic and copies ran while one was open for 4% of the time, Pallas kernels for 0%

profile of v1, /device:TPU:0, one launch (start us, length us, event | category | flops | bytes accessed | tf_op | source)
XLA Modules:
  0.0 48.0 jit_solution(13291038159662819638)
XLA Ops:
  0.6 0.6 %collective-permute-start = (f32[16,1024]{1,0:T(8,128)}, f32[16,1024]{1,0:T(8,128)S(1)}, u32[]{:S(2)}, u32[]{:S(2)}) collective-permute-start(f32[16,1024]{1,0:T(8,128)} %param.6), channel_id=1, source_target_pairs={{0,1},{1,0},{2,3},{3,2},{4,5},{5,4},{6,7},{7,6},{8,9},{9,8},{10,11... | collective-permute-start | bytes 196616 | tf_op jit(solution)/shard_map/ppermute | solution.py:246
  1.2 0.9 %slice_bitcast_fusion.1 = (f32[1,2048]{1,0:T(1,128)S(1)}, f32[1,2048]{1,0:T(1,128)S(1)}) fusion(f32[1,16,2048]{2,1,0:T(8,128)} %param.7), kind=kLoop, calls=%fused_computation.21 | loop fusion | bytes 32768 | tf_op jit(solution)/shard_map/slice | solution.py:253
  2.1 0.0 copy-start.1
  2.1 0.9 %bitcast_convert_fusion = f32[16,2048]{1,0:T(8,128)S(1)} fusion(s32[1,16,2048]{2,1,0:T(8,128)} %param.8), kind=kLoop, calls=%fused_computation.22 | loop fusion | flops 32768 | bytes 262144 | tf_op jit(solution)/shard_map/convert_element_type | solution.py:250
  3.1 0.0 collective-permute-done
  3.1 0.0 copy-done.1
  3.2 4.4 %collective-permute-start.1 = (f32[12,2048]{1,0:T(8,128)S(1)}, f32[12,2048]{1,0:T(8,128)S(1)}, u32[]{:S(2)}, u32[]{:S(2)}) collective-permute-start(f32[12,2048]{1,0:T(8,128)S(1)} %pad_maximum_fusion), channel_id=1, source_target_pairs={{0,2},{2,4},{4,6},{6,8},{8,10},{10,12},{12,14},{1,3},{3,5},{5,7},{... | collective-permute-start | bytes 294920 | tf_op jit(solution)/shard_map/ppermute | solution.py:253
  7.6 1.3 %collective-permute-start.2 = (f32[12,2048]{1,0:T(8,128)S(1)}, f32[12,2048]{1,0:T(8,128)S(1)}, u32[]{:S(2)}, u32[]{:S(2)}) collective-permute-start(f32[12,2048]{1,0:T(8,128)S(1)} %fusion.4), channel_id=1, source_target_pairs={{2,0},{4,2},{6,4},{8,6},{10,8},{12,10},{14,12},{3,1},{5,3},{7,5},{... | collective-permute-start | bytes 294920 | tf_op jit(solution)/shard_map/ppermute | solution.py:254
  8.9 0.1 pad.12.clone
  9.0 2.0 %collective-permute-done.1 = f32[12,2048]{1,0:T(8,128)S(1)} collective-permute-done((f32[12,2048]{1,0:T(8,128)S(1)}, f32[12,2048]{1,0:T(8,128)S(1)}, u32[]{:S(2)}, u32[]{:S(2)}) %collective-permute-start.1) | collective-permute-done | bytes 98336 | tf_op jit(solution)/shard_map/ppermute | solution.py:253
  11.0 4.2 %collective-permute-done.2 = f32[12,2048]{1,0:T(8,128)S(1)} collective-permute-done((f32[12,2048]{1,0:T(8,128)S(1)}, f32[12,2048]{1,0:T(8,128)S(1)}, u32[]{:S(2)}, u32[]{:S(2)}) %collective-permute-start.2) | collective-permute-done | bytes 98336 | tf_op jit(solution)/shard_map/ppermute | solution.py:254
  15.1 0.8 %select_maximum_fusion.ext_ref = f32[48,2304]{1,0:T(8,128)} fusion(f32[10,2048]{1,0:T(8,128)S(1)} %bitcast.14, f32[10,2048]{1,0:T(8,128)S(1)} %bitcast.13, f32[16,1024]{1,0:T(8,128)S(1)} %get-tuple-element.15, f32[16,1024]{1,0:T(8,128)S(1)} %get-tuple-element.14), kind=kLoop, calls=%fused_computation.4 | loop fusion | flops 1990656 | bytes 737280 | tf_op jit(solution)/shard_map/concatenate | solution.py:257
  15.9 6.4 %normal.1.local_ref = f32[72,128]{1,0:T(8,128)} custom-call(f32[48,2304]{1,0:T(8,128)} %select_maximum_fusion.ext_ref, f32[16,2048]{1,0:T(8,128)} %bitcast.10, s32[16,2048]{1,0:T(8,128)} %bitcast.12, s32[1,16]{1,0:T(1,128)} %blk_ref.1, f32[19,19]{1,0:T(8,128)} %rowf_ref.3, f32[19,19]{1,0:T(8,128)} %colf_ref.3), custom_call_target="tpu_custom_call" | custom-call | tf_op jit(solution)/shard_map/normal/pallas_call | solution.py:268
  22.3 0.0 copy-start
  22.3 20.0 %solve.1.coef_ref = f32[72,128]{1,0:T(8,128)} custom-call(f32[72,128]{1,0:T(8,128)} %normal.1.local_ref), custom_call_target="tpu_custom_call" | custom-call | tf_op jit(solution)/shard_map/solve/pallas_call | solution.py:281
  42.4 0.0 copy-done
  42.4 0.9 %maximum_maximum_fusion.1 = (f32[24,2048]{1,0:T(8,128)}, f32[24,2048]{1,0:T(8,128)}) fusion(f32[1,2048]{1,0:T(1,128)S(1)} %get-tuple-element.8, f32[16,2048]{1,0:T(8,128)S(1)} %bitcast_convert_fusion, f32[1,2048]{1,0:T(1,128)S(1)} %get-tuple-element.6, f32[24]{0:T(128)S(1)} %pad.12.clone, f32[1,2048]{1,0:T(1,128)S(1)} %get-tuple-element.9, ...), kind=kLoop, calls=%fused_computation.11 | loop fusion | flops 294912 | bytes 688224 | tf_op jit(solution)/shard_map/concatenate | solution.py:263
  43.2 4.8 %model.1 = (f32[16,2048]{1,0:T(8,128)}, f32[1,64]{1,0:T(1,128)}) custom-call(f32[72,128]{1,0:T(8,128)} %solve.1.coef_ref, f32[48,2304]{1,0:T(8,128)} %select_maximum_fusion.ext_ref, f32[24,2048]{1,0:T(8,128)} %get-tuple-element.17.exp_ref, f32[24,2048]{1,0:T(8,128)} %get-tuple-element.16.mask_ref, f32[19,19]{1,0:T(8,128)} %rowf_ref.3, f32[19,19]{1,0:T(8,128)} %colf_ref.3), custom_call_target="tpu_custom_call" | custom-call | tf_op jit(solution)/shard_map/model/pallas_call | solution.py:295
  (8 shorter events, 0.1 us)
Async XLA Ops:
  0.6 2.4 %collective-permute-start = (f32[16,1024]{1,0:T(8,128)}, f32[16,1024]{1,0:T(8,128)S(1)}, u32[]{:S(2)}, u32[]{:S(2)}) collective-permute-start(f32[16,1024]{1,0:T(8,128)} %param.6), channel_id=1, source_target_pairs={{0,1},{1,0},{2,3},{3,2},{4,5},{5,4},{6,7},{7,6},{8,9},{9,8},{10,11... | collective-permute-start | bytes 196616 | tf_op jit(solution)/shard_map/ppermute | solution.py:246
  2.1 1.0 %copy-start.1 = (f32[16,1024]{1,0:T(8,128)S(1)}, f32[16,1024]{1,0:T(8,128)}, u32[]{:S(2)}) copy-start(f32[16,1024]{1,0:T(8,128)} %param.6) | copy-start | bytes 196612
  3.2 7.8 %collective-permute-start.1 = (f32[12,2048]{1,0:T(8,128)S(1)}, f32[12,2048]{1,0:T(8,128)S(1)}, u32[]{:S(2)}, u32[]{:S(2)}) collective-permute-start(f32[12,2048]{1,0:T(8,128)S(1)} %pad_maximum_fusion), channel_id=1, source_target_pairs={{0,2},{2,4},{4,6},{6,8},{8,10},{10,12},{12,14},{1,3},{3,5},{5,7},{... | collective-permute-start | bytes 294920 | tf_op jit(solution)/shard_map/ppermute | solution.py:253
  7.6 7.5 %collective-permute-start.2 = (f32[12,2048]{1,0:T(8,128)S(1)}, f32[12,2048]{1,0:T(8,128)S(1)}, u32[]{:S(2)}, u32[]{:S(2)}) collective-permute-start(f32[12,2048]{1,0:T(8,128)S(1)} %fusion.4), channel_id=1, source_target_pairs={{2,0},{4,2},{6,4},{8,6},{10,8},{12,10},{14,12},{3,1},{5,3},{7,5},{... | collective-permute-start | bytes 294920 | tf_op jit(solution)/shard_map/ppermute | solution.py:254
  22.3 20.0 %copy-start = (f32[1,16,2048]{2,1,0:T(8,128)S(1)}, f32[1,16,2048]{2,1,0:T(8,128)}, u32[]{:S(2)}) copy-start(f32[1,16,2048]{2,1,0:T(8,128)} %param.7) | copy-start | bytes 393220

commit v2 on v1

--- a/solution.py
+++ b/solution.py
@@ -178,11 +178,11 @@
     out_ref[:fit, :] = answer
 
 
-def model_kernel(region_rows, coef_ref, ext_ref, exp_ref, mask_ref, rowf_ref, colf_ref, out_ref, row_ref, band, wide_y, diff):
+def model_kernel(region_rows, coef_ref, ext_ref, exp_ref, mask_ref, edge_ref, rowf_ref, colf_ref, out_ref, row_ref, band, wide_y, diff):
     rows, cols = out_ref.shape
     bases, taps = rowf_ref.shape
     fit = 3 * bases + 7
-    tall = exp_ref.shape[0]
+    tall = diff.shape[0]
     answer = coef_ref[:fit, :fit]
     same = lax.broadcasted_iota(jnp.int32, (fit, fit), 0) == lax.broadcasted_iota(jnp.int32, (fit, fit), 1)
     row_ref[...] = jnp.sum(jnp.where(same, answer, 0.0), axis=0, keepdims=True)
@@ -225,8 +225,12 @@
     for j in range(taps):
         y = wide_y[j * tall : (j + 1) * tall, :]
         model = model + pltpu.roll(y, wide - (EDGE - HALF) - j, 1)[:, :cols]
-    d = mask_ref[...] * (exp_ref[...] - model)
-    diff[...] = d
+    spare = jnp.zeros((tall - rows - 2, cols), jnp.float32)
+    science = jnp.concatenate([edge_ref[0, 0:1, :], exp_ref[...], edge_ref[1, 0:1, :], spare], axis=0)
+    good = jnp.concatenate(
+        [edge_ref[0, 1:2, :], mask_ref[...].astype(jnp.float32), edge_ref[1, 1:2, :], spare], axis=0
+    )
+    diff[...] = good * (science - model)
     lane = lax.broadcasted_iota(jnp.int32, (rows, cols), 1)
     mid = diff[1 : rows + 1, :]
     left = jnp.where(lane == 0, 0.0, pltpu.roll(mid, 1, 1))
@@ -235,36 +239,137 @@
     out_ref[...] = 4.0 * mid - around
 
 
+def halo_kernel(count, tmpl_ref, exp_ref, mask_ref, ext_ref, edge_ref, parts, edge_send, edge_recv, send_sem, recv_sem):
+    me = lax.axis_index("stripe")
+    core = lax.axis_index("exp")
+    rows, half = tmpl_ref.shape
+    has_up = me > 0
+    has_down = me < count - 1
+
+    def copy(src, dst, n, stripe, exp):
+        return pltpu.make_async_remote_copy(
+            src_ref=src,
+            dst_ref=dst,
+            send_sem=send_sem.at[n],
+            recv_sem=recv_sem.at[n],
+            device_id={"stripe": stripe, "exp": exp},
+            device_id_type=MESH,
+        )
+
+    def downs():
+        return [
+            copy(edge_send.at[0], edge_recv.at[0], 2, me + 1, core),
+            copy(tmpl_ref, parts.at[0], 0, me + 1, core),
+            copy(tmpl_ref, parts.at[1], 1, me + 1, 1 - core),
+        ]
+
+    def ups():
+        return [
+            copy(edge_send.at[1], edge_recv.at[1], 5, me - 1, core),
+            copy(tmpl_ref, parts.at[2], 3, me - 1, core),
+            copy(tmpl_ref, parts.at[3], 4, me - 1, 1 - core),
+        ]
+
+    edge_send[0, 0:1, :] = exp_ref[rows - 1 : rows, :]
+    edge_send[0, 1:2, :] = mask_ref[rows - 1 : rows, :].astype(jnp.float32)
+    edge_send[1, 0:1, :] = exp_ref[0:1, :]
+    edge_send[1, 1:2, :] = mask_ref[0:1, :].astype(jnp.float32)
+    barrier = pltpu.get_barrier_semaphore()
+
+    def greet(stripe, exp):
+        pl.semaphore_signal(barrier, inc=1, device_id={"stripe": stripe, "exp": exp}, device_id_type=MESH)
+
+    @pl.when(has_up)
+    def _():
+        greet(me - 1, core)
+        greet(me - 1, 1 - core)
+
+    @pl.when(has_down)
+    def _():
+        greet(me + 1, core)
+        greet(me + 1, 1 - core)
+
+    greet(me, 1 - core)
+    pl.semaphore_wait(barrier, 1 + 2 * has_up.astype(jnp.int32) + 2 * has_down.astype(jnp.int32))
+
+    @pl.when(has_down)
+    def _():
+        for c in downs():
+            c.start()
+
+    @pl.when(has_up)
+    def _():
+        for c in ups():
+            c.start()
+
+    across = copy(tmpl_ref, parts.at[4], 6, me, 1 - core)
+    across.start()
+    ext_ref[...] = jnp.zeros_like(ext_ref)
+    edge_ref[...] = jnp.zeros_like(edge_ref)
+    mine = pl.ds(pl.multiple_of(EDGE + core * half, EDGE), half)
+    theirs = pl.ds(pl.multiple_of(EDGE + (1 - core) * half, EDGE), half)
+    ext_ref[rows : 2 * rows, mine] = tmpl_ref[...]
+    across.wait()
+    ext_ref[rows : 2 * rows, theirs] = parts[4]
+
+    @pl.when(has_up)
+    def _():
+        for c in downs():
+            c.wait_recv()
+        edge_ref[0] = edge_recv[0]
+        ext_ref[0:rows, mine] = parts[0]
+        ext_ref[0:rows, theirs] = parts[1]
+
+    @pl.when(has_down)
+    def _():
+        for c in ups():
+            c.wait_recv()
+        edge_ref[1] = edge_recv[1]
+        ext_ref[2 * rows : 3 * rows, mine] = parts[2]
+        ext_ref[2 * rows : 3 * rows, theirs] = parts[3]
+
+    @pl.when(has_down)
+    def _():
+        for c in downs():
+            c.wait_send()
+
+    @pl.when(has_up)
+    def _():
+        for c in ups():
+            c.wait_send()
+
+
 def shards(template, exposure, cosmic_mask, stamp_blocks, row_filters, col_filters):
     rows, cols = exposure.shape[1:]
     bases, taps = row_filters.shape
     fit = 3 * bases + 7
-    reach = HALF + 1
     stripes = lax.axis_size("stripe")
     region_rows = rows * stripes
-    me_exp = lax.axis_index("exp")
-    other = lax.ppermute(template, "exp", [(0, 1), (1, 0)])
-    is_first = me_exp == 0
-    full = jnp.concatenate([jnp.where(is_first, template, other), jnp.where(is_first, other, template)], axis=1)
     own_exp = exposure[0]
-    own_mask = cosmic_mask[0].astype(jnp.float32)
-    down = [(i, i + 1) for i in range(stripes - 1)]
-    up = [(i + 1, i) for i in range(stripes - 1)]
-    above = lax.ppermute(jnp.concatenate([full[rows - reach :], own_exp[rows - 1 :], own_mask[rows - 1 :]]), "stripe", down)
-    below = lax.ppermute(jnp.concatenate([full[:reach], own_exp[:1], own_mask[:1]]), "stripe", up)
-    side = round_up(reach, 16)
-    ext_rows = rows + 2 * side
-    ext = jnp.concatenate([above[:reach], full, below[:reach]], axis=0)
-    ext = jnp.pad(ext, ((side - reach, side - reach), (EDGE, EDGE)))
-    wide = ext.shape[1]
+    own_mask = cosmic_mask[0]
+    half = template.shape[1]
+    ext_rows = 3 * rows
+    wide = cols + 2 * EDGE
     tall = round_up(rows + 2, 8)
-    spare = jnp.zeros((tall - rows - 2, cols), jnp.float32)
-    exp_tall = jnp.concatenate([above[reach : reach + 1], own_exp, below[reach : reach + 1], spare])
-    mask_tall = jnp.concatenate([above[reach + 1 :], own_mask, below[reach + 1 :], spare])
     total = round_up(fit + 1, 8)
     vmem = pl.BlockSpec(memory_space=pltpu.VMEM)
     smem = pl.BlockSpec(memory_space=pltpu.SMEM)
     f32 = jnp.float32
+    ext, edges = pl.pallas_call(
+        functools.partial(halo_kernel, stripes),
+        out_shape=(jax.ShapeDtypeStruct((ext_rows, wide), f32), jax.ShapeDtypeStruct((2, 2, cols), f32)),
+        in_specs=[vmem] * 3,
+        out_specs=(vmem, vmem),
+        scratch_shapes=[
+            pltpu.VMEM((5, rows, half), f32),
+            pltpu.VMEM((2, 2, cols), f32),
+            pltpu.VMEM((2, 2, cols), f32),
+            pltpu.SemaphoreType.DMA((7,)),
+            pltpu.SemaphoreType.DMA((7,)),
+        ],
+        compiler_params=pltpu.CompilerParams(collective_id=1, has_side_effects=True),
+        name="halo",
+    )(template, own_exp, own_mask)
     normal = pl.pallas_call(
         functools.partial(normal_kernel, float(region_rows)),
         out_shape=jax.ShapeDtypeStruct((total, EDGE), f32),
@@ -276,7 +381,7 @@
             pltpu.VMEM((cols // (2 * EDGE), total * rows, EDGE), f32),
         ],
         name="normal",
-    )(ext, own_exp, cosmic_mask[0], stamp_blocks, row_filters, col_filters)
+    )(ext, own_exp, own_mask, stamp_blocks, row_filters, col_filters)
     hops = max(1, (stripes - 1).bit_length())
     coef = pl.pallas_call(
         functools.partial(solve_kernel, stripes, fit),
@@ -295,7 +400,7 @@
     filtered, coef_row = pl.pallas_call(
         functools.partial(model_kernel, float(region_rows)),
         out_shape=(jax.ShapeDtypeStruct((rows, cols), f32), jax.ShapeDtypeStruct((1, fit), f32)),
-        in_specs=[vmem] * 6,
+        in_specs=[vmem] * 7,
         out_specs=(vmem, vmem),
         scratch_shapes=[
             pltpu.VMEM((taps * tall, EDGE), f32),
@@ -303,7 +408,7 @@
             pltpu.VMEM((tall, cols), f32),
         ],
         name="model",
-    )(coef, ext, exp_tall, mask_tall, row_filters, col_filters)
+    )(coef, ext, own_exp, own_mask, edges, row_filters, col_filters)
     return (filtered[None], coef_row)
 
 

time: 48.3 us -> 43.1 us (0.89)
  Pallas kernels: 31.2 us -> 42.2 us
  starting transfers between devices: 6.26 us -> 0 us
  waiting for transfers between devices: 6.12 us -> 0 us
  other arithmetic: 2.7 us -> 0 us
  local copies, waits for them, and re-layouts: 1.02 us -> 0 us
    pallas_call x0 -> x1, Pallas kernels: none -> 11.7 us  [shards(): pl.pallas_call(functools.partial(halo_kernel, stripes), out_shape=(jax.Sh...]
    ppermute x3 -> x0, starting transfers between devices: 6.26 us -> none  [the longest x1 4.41 us: shards(): lax.ppermute(jnp.concatenate([full[rows - reach:], own_exp[rows - 1:], ow...]
    ppermute x3 -> x0, waiting for transfers between devices: 6.12 us -> none  [the longest x1 4.16 us: shards(): lax.ppermute(jnp.concatenate([full[:reach], own_exp[:1], own_mask[:1]]),...]
    concatenate x5 -> x0, other arithmetic: 1.74 us -> none  [the longest x1 0.86 us: shards(): jnp.concatenate([above[reach + 1:], own_mask, below[reach + 1:], spare])]
    convert_element_type x1 -> x0, other arithmetic: 0.95 us -> none  [shards(): own_mask = cosmic_mask[0].astype(jnp.float32)]
    slice x4 -> x0, local copies, waits for them, and re-layouts: 0.93 us -> none  [the longest x1 0.88 us: shards(): own_exp[rows - 1:]]
    pallas_call x1, Pallas kernels: 20 us -> 19.4 us  [shards(): pl.pallas_call(functools.partial(solve_kernel, stripes, fit), out_shape=j...]
  transfers between devices with their start and end apart: 3 -> 0, of which waited for: 2 -> 0; matrix products, arithmetic and copies ran while one was open for 4% -> 0% of each run, Pallas kernels for 0% -> 0%
where the time goes in v2:
time: 43.1 us; the launch traced here: 42.9 us
  Pallas kernels  42.2 us (98%)
  between operations  0.65 us (2%)
    pallas_call x1, Pallas kernels, shards(): pl.pallas_call(functools.partial(solve_kernel, stripes, fit), out_shape=j...  19.4 us
    pallas_call x1, Pallas kernels, shards(): pl.pallas_call(functools.partial(halo_kernel, stripes), out_shape=(jax.Sh...  11.7 us
    pallas_call x1, Pallas kernels, shards(): pl.pallas_call(functools.partial(normal_kernel, float(region_rows)), out_...  6.43 us
    pallas_call x1, Pallas kernels, shards(): pl.pallas_call(functools.partial(model_kernel, float(region_rows)), out_s...  4.75 us

profile of v2, /device:TPU:0, one launch (start us, length us, event | category | flops | bytes accessed | tf_op | source)
XLA Modules:
  0.0 42.9 jit_solution(14914942562055912735)
XLA Ops:
  0.6 11.7 %halo.1 = (f32[48,2304]{1,0:T(8,128)}, f32[2,2,2048]{2,1,0:T(2,128)}) custom-call(f32[16,1024]{1,0:T(8,128)} %tmpl_ref.1, f32[16,2048]{1,0:T(8,128)} %bitcast.3, s32[16,2048]{1,0:T(8,128)} %bitcast.6), custom_call_target="tpu_custom_call" | custom-call | tf_op jit(solution)/shard_map/halo/pallas_call | solution.py:358
  12.3 6.4 %normal.1.local_ref = f32[72,128]{1,0:T(8,128)} custom-call(f32[48,2304]{1,0:T(8,128)} %get-tuple-element.6.ext_ref, f32[16,2048]{1,0:T(8,128)} %bitcast.4, s32[16,2048]{1,0:T(8,128)} %bitcast.7, s32[1,16]{1,0:T(1,128)} %blk_ref.1, f32[19,19]{1,0:T(8,128)} %rowf_ref.3, f32[19,19]{1,0:T(8,128)} %colf_ref.3), custom_call_target="tpu_custom_call" | custom-call | tf_op jit(solution)/shard_map/normal/pallas_call | solution.py:373
  18.8 19.4 %solve.1.coef_ref = f32[72,128]{1,0:T(8,128)} custom-call(f32[72,128]{1,0:T(8,128)} %normal.1.local_ref), custom_call_target="tpu_custom_call" | custom-call | tf_op jit(solution)/shard_map/solve/pallas_call | solution.py:386
  38.1 4.7 %model.1 = (f32[16,2048]{1,0:T(8,128)}, f32[1,64]{1,0:T(1,128)}) custom-call(f32[72,128]{1,0:T(8,128)} %solve.1.coef_ref, f32[48,2304]{1,0:T(8,128)} %get-tuple-element.6.ext_ref, f32[16,2048]{1,0:T(8,128)} %bitcast.5, s32[16,2048]{1,0:T(8,128)} %bitcast.8, f32[2,2,2048]{2,1,0:T(2,128)} %get-tuple-element.7.edge_ref, f32[19,19]{1,0:T(8,128)} %rowf_ref.3, ...), custom_call_target="tpu_custom_call" | custom-call | tf_op jit(solution)/shard_map/model/pallas_call | solution.py:400

commit v3 on v2

--- a/solution.py
+++ b/solution.py
@@ -10,6 +10,8 @@
 HALF = 9
 STAMP_W = 64
 EDGE = 128
+TILE = 8
+BLOCK = 4
 HIGHEST = lax.Precision.HIGHEST
 MESH = pl.DeviceIdType.MESH
 
@@ -169,10 +171,16 @@
         total = total + held[s]
     a = total[:fit, :]
     sub = lax.broadcasted_iota(jnp.int32, a.shape, 0)
-    for k in range(fit):
-        row = a[k : k + 1, :]
-        row = row * pl.reciprocal(jnp.broadcast_to(a[k : k + 1, k : k + 1], row.shape))
-        a = jnp.where(sub == k, row, a - a[:, k : k + 1] * row)
+    for first in range(0, fit, BLOCK):
+        block = range(first, min(first + BLOCK, fit))
+        cols = [jnp.broadcast_to(a[:, k : k + 1], a.shape) for k in block]
+        for t, k in enumerate(block):
+            inverse = pl.reciprocal(cols[t][k : k + 1, :])
+            row = a[k : k + 1, :] * inverse
+            a = jnp.where(sub == k, row, a - cols[t] * row)
+            for w in range(t + 1, len(block)):
+                factor = cols[w][k : k + 1, :] * inverse
+                cols[w] = jnp.where(sub == k, factor, cols[w] - cols[t] * factor)
     answer = jnp.broadcast_to(a[:, fit : fit + 1], a.shape)
     out_ref[...] = jnp.zeros_like(out_ref)
     out_ref[:fit, :] = answer
@@ -239,7 +247,7 @@
     out_ref[...] = 4.0 * mid - around
 
 
-def halo_kernel(count, tmpl_ref, exp_ref, mask_ref, ext_ref, edge_ref, parts, edge_send, edge_recv, send_sem, recv_sem):
+def halo_kernel(count, tmpl_ref, exp_ref, mask_ref, ext_ref, edge_ref, parts, whole, extra_send, extra_recv, edge_send, edge_recv, send_sem, recv_sem):
     me = lax.axis_index("stripe")
     core = lax.axis_index("exp")
     rows, half = tmpl_ref.shape
@@ -256,20 +264,25 @@
             device_id_type=MESH,
         )
 
+    def sends(way, stripe, tile):
+        base = 5 * way
+        return [
+            copy(edge_send.at[way], edge_recv.at[way], base, stripe, core),
+            copy(extra_send.at[way], extra_recv.at[2 * way], base + 1, stripe, core),
+            copy(extra_send.at[way], extra_recv.at[2 * way + 1], base + 2, stripe, 1 - core),
+            copy(tile, parts.at[2 * way], base + 3, stripe, core),
+            copy(tile, parts.at[2 * way + 1], base + 4, stripe, 1 - core),
+        ]
+
     def downs():
-        return [
-            copy(edge_send.at[0], edge_recv.at[0], 2, me + 1, core),
-            copy(tmpl_ref, parts.at[0], 0, me + 1, core),
-            copy(tmpl_ref, parts.at[1], 1, me + 1, 1 - core),
-        ]
+        return sends(0, me + 1, tmpl_ref.at[rows - TILE : rows])
 
     def ups():
-        return [
-            copy(edge_send.at[1], edge_recv.at[1], 5, me - 1, core),
-            copy(tmpl_ref, parts.at[2], 3, me - 1, core),
-            copy(tmpl_ref, parts.at[3], 4, me - 1, 1 - core),
-        ]
-
+        return sends(1, me - 1, tmpl_ref.at[0:TILE])
+
+    more = HALF + 1 - TILE
+    extra_send[0] = tmpl_ref[rows - TILE - more : rows - TILE, :]
+    extra_send[1] = tmpl_ref[TILE : TILE + more, :]
     edge_send[0, 0:1, :] = exp_ref[rows - 1 : rows, :]
     edge_send[0, 1:2, :] = mask_ref[rows - 1 : rows, :].astype(jnp.float32)
     edge_send[1, 0:1, :] = exp_ref[0:1, :]
@@ -302,7 +315,7 @@
         for c in ups():
             c.start()
 
-    across = copy(tmpl_ref, parts.at[4], 6, me, 1 - core)
+    across = copy(tmpl_ref, whole, 10, me, 1 - core)
     across.start()
     ext_ref[...] = jnp.zeros_like(ext_ref)
     edge_ref[...] = jnp.zeros_like(edge_ref)
@@ -310,23 +323,25 @@
     theirs = pl.ds(pl.multiple_of(EDGE + (1 - core) * half, EDGE), half)
     ext_ref[rows : 2 * rows, mine] = tmpl_ref[...]
     across.wait()
-    ext_ref[rows : 2 * rows, theirs] = parts[4]
+    ext_ref[rows : 2 * rows, theirs] = whole[...]
 
     @pl.when(has_up)
     def _():
         for c in downs():
             c.wait_recv()
         edge_ref[0] = edge_recv[0]
-        ext_ref[0:rows, mine] = parts[0]
-        ext_ref[0:rows, theirs] = parts[1]
+        for n, lanes in enumerate((mine, theirs)):
+            ext_ref[rows - TILE : rows, lanes] = parts[n]
+            ext_ref[rows - TILE - more : rows - TILE, lanes] = extra_recv[n]
 
     @pl.when(has_down)
     def _():
         for c in ups():
             c.wait_recv()
         edge_ref[1] = edge_recv[1]
-        ext_ref[2 * rows : 3 * rows, mine] = parts[2]
-        ext_ref[2 * rows : 3 * rows, theirs] = parts[3]
+        for n, lanes in enumerate((mine, theirs)):
+            ext_ref[2 * rows : 2 * rows + TILE, lanes] = parts[2 + n]
+            ext_ref[2 * rows + TILE : 2 * rows + TILE + more, lanes] = extra_recv[2 + n]
 
     @pl.when(has_down)
     def _():
@@ -361,11 +376,14 @@
         in_specs=[vmem] * 3,
         out_specs=(vmem, vmem),
         scratch_shapes=[
-            pltpu.VMEM((5, rows, half), f32),
+            pltpu.VMEM((4, TILE, half), f32),
+            pltpu.VMEM((rows, half), f32),
+            pltpu.VMEM((2, HALF + 1 - TILE, half), f32),
+            pltpu.VMEM((4, HALF + 1 - TILE, half), f32),
             pltpu.VMEM((2, 2, cols), f32),
             pltpu.VMEM((2, 2, cols), f32),
-            pltpu.SemaphoreType.DMA((7,)),
-            pltpu.SemaphoreType.DMA((7,)),
+            pltpu.SemaphoreType.DMA((11,)),
+            pltpu.SemaphoreType.DMA((11,)),
         ],
         compiler_params=pltpu.CompilerParams(collective_id=1, has_side_effects=True),
         name="halo",

time: 43.1 us -> 38.3 us (0.89)
  Pallas kernels: 42.2 us -> 37.4 us
    pallas_call x1, Pallas kernels: 19.4 us -> 16.5 us  [shards(): pl.pallas_call(functools.partial(solve_kernel, stripes, fit), out_shape=j...]
    pallas_call x1, Pallas kernels: 11.7 us -> 9.69 us  [shards(): pl.pallas_call(functools.partial(halo_kernel, stripes), out_shape=(jax.Sh...]
where the time goes in v3:
time: 38.3 us; the launch traced here: 38 us
  Pallas kernels  37.4 us (98%)
  between operations  0.65 us (2%)
    pallas_call x1, Pallas kernels, shards(): pl.pallas_call(functools.partial(solve_kernel, stripes, fit), out_shape=j...  16.5 us
    pallas_call x1, Pallas kernels, shards(): pl.pallas_call(functools.partial(halo_kernel, stripes), out_shape=(jax.Sh...  9.69 us
    pallas_call x1, Pallas kernels, shards(): pl.pallas_call(functools.partial(normal_kernel, float(region_rows)), out_...  6.42 us
    pallas_call x1, Pallas kernels, shards(): pl.pallas_call(functools.partial(model_kernel, float(region_rows)), out_s...  4.75 us

profile of v3, /device:TPU:0, one launch (start us, length us, event | category | flops | bytes accessed | tf_op | source)
XLA Modules:
  0.0 38.0 jit_solution(12082885294863672440)
XLA Ops:
  0.6 9.7 %halo.1 = (f32[48,2304]{1,0:T(8,128)}, f32[2,2,2048]{2,1,0:T(2,128)}) custom-call(f32[16,1024]{1,0:T(8,128)} %tmpl_ref.1, f32[16,2048]{1,0:T(8,128)} %bitcast.3, s32[16,2048]{1,0:T(8,128)} %bitcast.6), custom_call_target="tpu_custom_call" | custom-call | tf_op jit(solution)/shard_map/halo/pallas_call | solution.py:373
  10.3 6.4 %normal.1.local_ref = f32[72,128]{1,0:T(8,128)} custom-call(f32[48,2304]{1,0:T(8,128)} %get-tuple-element.6.ext_ref, f32[16,2048]{1,0:T(8,128)} %bitcast.4, s32[16,2048]{1,0:T(8,128)} %bitcast.7, s32[1,16]{1,0:T(1,128)} %blk_ref.1, f32[19,19]{1,0:T(8,128)} %rowf_ref.3, f32[19,19]{1,0:T(8,128)} %colf_ref.3), custom_call_target="tpu_custom_call" | custom-call | tf_op jit(solution)/shard_map/normal/pallas_call | solution.py:391
  16.8 16.5 %solve.1.coef_ref = f32[72,128]{1,0:T(8,128)} custom-call(f32[72,128]{1,0:T(8,128)} %normal.1.local_ref), custom_call_target="tpu_custom_call" | custom-call | tf_op jit(solution)/shard_map/solve/pallas_call | solution.py:404
  33.3 4.8 %model.1 = (f32[16,2048]{1,0:T(8,128)}, f32[1,64]{1,0:T(1,128)}) custom-call(f32[72,128]{1,0:T(8,128)} %solve.1.coef_ref, f32[48,2304]{1,0:T(8,128)} %get-tuple-element.6.ext_ref, f32[16,2048]{1,0:T(8,128)} %bitcast.5, s32[16,2048]{1,0:T(8,128)} %bitcast.8, f32[2,2,2048]{2,1,0:T(2,128)} %get-tuple-element.7.edge_ref, f32[19,19]{1,0:T(8,128)} %rowf_ref.3, ...), custom_call_target="tpu_custom_call" | custom-call | tf_op jit(solution)/shard_map/model/pallas_call | solution.py:418

commit v4 on v3

--- a/solution.py
+++ b/solution.py
@@ -11,7 +11,7 @@
 STAMP_W = 64
 EDGE = 128
 TILE = 8
-BLOCK = 4
+BLOCK = 8
 HIGHEST = lax.Precision.HIGHEST
 MESH = pl.DeviceIdType.MESH
 
@@ -140,7 +140,26 @@
     out_ref[...] = jnp.concatenate([acc, jnp.zeros((total, EDGE - total), jnp.float32)], axis=1)
 
 
-def solve_kernel(count, fit, local_ref, out_ref, send, held, send_sem, recv_sem):
+def fit_kernel(
+    count,
+    fit,
+    region_rows,
+    ext_ref,
+    exp_ref,
+    mask_ref,
+    blk_ref,
+    rowf_ref,
+    colf_ref,
+    out_ref,
+    local_ref,
+    bandw,
+    vert,
+    design,
+    send,
+    held,
+    send_sem,
+    recv_sem,
+):
     me = lax.axis_index("stripe")
     steps = []
     d = 1
@@ -151,6 +170,9 @@
     barrier = pltpu.get_barrier_semaphore()
     for partner in partners:
         pl.semaphore_signal(barrier, inc=1, device_id={"stripe": partner}, device_id_type=MESH)
+    normal_kernel(
+        region_rows, ext_ref, exp_ref, mask_ref, blk_ref, rowf_ref, colf_ref, local_ref, bandw, vert, design
+    )
     pl.semaphore_wait(barrier, len(partners))
     total = local_ref[...]
     for s, partner in enumerate(partners):
@@ -388,33 +410,25 @@
         compiler_params=pltpu.CompilerParams(collective_id=1, has_side_effects=True),
         name="halo",
     )(template, own_exp, own_mask)
-    normal = pl.pallas_call(
-        functools.partial(normal_kernel, float(region_rows)),
+    hops = max(1, (stripes - 1).bit_length())
+    coef = pl.pallas_call(
+        functools.partial(fit_kernel, stripes, fit, float(region_rows)),
         out_shape=jax.ShapeDtypeStruct((total, EDGE), f32),
         in_specs=[vmem] * 3 + [smem] + [vmem] * 2,
         out_specs=vmem,
         scratch_shapes=[
+            pltpu.VMEM((total, EDGE), f32),
             pltpu.VMEM((bases * rows, 2 * EDGE), f32),
             pltpu.VMEM((bases * rows, cols), f32),
             pltpu.VMEM((cols // (2 * EDGE), total * rows, EDGE), f32),
-        ],
-        name="normal",
-    )(ext, own_exp, own_mask, stamp_blocks, row_filters, col_filters)
-    hops = max(1, (stripes - 1).bit_length())
-    coef = pl.pallas_call(
-        functools.partial(solve_kernel, stripes, fit),
-        out_shape=jax.ShapeDtypeStruct((total, EDGE), f32),
-        in_specs=[vmem],
-        out_specs=vmem,
-        scratch_shapes=[
             pltpu.VMEM((hops, total, EDGE), f32),
             pltpu.VMEM((hops, total, EDGE), f32),
             pltpu.SemaphoreType.DMA((hops,)),
             pltpu.SemaphoreType.DMA((hops,)),
         ],
         compiler_params=pltpu.CompilerParams(collective_id=0, has_side_effects=True),
-        name="solve",
-    )(normal)
+        name="fit",
+    )(ext, own_exp, own_mask, stamp_blocks, row_filters, col_filters)
     filtered, coef_row = pl.pallas_call(
         functools.partial(model_kernel, float(region_rows)),
         out_shape=(jax.ShapeDtypeStruct((rows, cols), f32), jax.ShapeDtypeStruct((1, fit), f32)),

time: 38.3 us -> 33.9 us (0.89)
  Pallas kernels: 37.4 us -> 33 us
    pallas_call x2 -> x1, Pallas kernels: 23 us -> 18.6 us  [shards(): pl.pallas_call(functools.partial(fit_kernel, stripes, fit, float(region_r...]
where the time goes in v4:
time: 33.9 us; the launch traced here: 33.7 us
  Pallas kernels  33 us (97%)
  between operations  0.64 us (2%)
    pallas_call x1, Pallas kernels, shards(): pl.pallas_call(functools.partial(fit_kernel, stripes, fit, float(region_r...  18.6 us
    pallas_call x1, Pallas kernels, shards(): pl.pallas_call(functools.partial(halo_kernel, stripes), out_shape=(jax.Sh...  9.69 us
    pallas_call x1, Pallas kernels, shards(): pl.pallas_call(functools.partial(model_kernel, float(region_rows)), out_s...  4.75 us

profile of v4, /device:TPU:0, one launch (start us, length us, event | category | flops | bytes accessed | tf_op | source)
XLA Modules:
  0.0 33.7 jit_solution(12545621019187294969)
XLA Ops:
  0.6 9.7 %halo.1 = (f32[48,2304]{1,0:T(8,128)}, f32[2,2,2048]{2,1,0:T(2,128)}) custom-call(f32[16,1024]{1,0:T(8,128)} %tmpl_ref.1, f32[16,2048]{1,0:T(8,128)} %bitcast.3, s32[16,2048]{1,0:T(8,128)} %bitcast.6), custom_call_target="tpu_custom_call" | custom-call | tf_op jit(solution)/shard_map/halo/pallas_call | solution.py:395
  10.3 18.6 %fit.1.coef_ref = f32[72,128]{1,0:T(8,128)} custom-call(f32[48,2304]{1,0:T(8,128)} %get-tuple-element.6.ext_ref, f32[16,2048]{1,0:T(8,128)} %bitcast.4, s32[16,2048]{1,0:T(8,128)} %bitcast.7, s32[1,16]{1,0:T(1,128)} %blk_ref.1, f32[19,19]{1,0:T(8,128)} %rowf_ref.3, f32[19,19]{1,0:T(8,128)} %colf_ref.3), custom_call_target="tpu_custom_call" | custom-call | tf_op jit(solution)/shard_map/fit/pallas_call | solution.py:414
  28.9 4.8 %model.1 = (f32[16,2048]{1,0:T(8,128)}, f32[1,64]{1,0:T(1,128)}) custom-call(f32[72,128]{1,0:T(8,128)} %fit.1.coef_ref, f32[48,2304]{1,0:T(8,128)} %get-tuple-element.6.ext_ref, f32[16,2048]{1,0:T(8,128)} %bitcast.5, s32[16,2048]{1,0:T(8,128)} %bitcast.8, f32[2,2,2048]{2,1,0:T(2,128)} %get-tuple-element.7.edge_ref, f32[19,19]{1,0:T(8,128)} %rowf_ref.3, ...), custom_call_target="tpu_custom_call" | custom-call | tf_op jit(solution)/shard_map/model/pallas_call | solution.py:432

commit v5 on v1

--- a/solution.py
+++ b/solution.py
@@ -10,6 +10,8 @@
 HALF = 9
 STAMP_W = 64
 EDGE = 128
+TILE = 8
+BLOCK = 8
 HIGHEST = lax.Precision.HIGHEST
 MESH = pl.DeviceIdType.MESH
 
@@ -138,7 +140,150 @@
     out_ref[...] = jnp.concatenate([acc, jnp.zeros((total, EDGE - total), jnp.float32)], axis=1)
 
 
-def solve_kernel(count, fit, local_ref, out_ref, send, held, send_sem, recv_sem):
+def exchange_halo(count, partners, tmpl_ref, exp_ref, mask_ref, ext_ref, edge_ref, parts, whole, extra_send, extra_recv, edge_send, edge_recv, send_sem, recv_sem):
+    me = lax.axis_index("stripe")
+    core = lax.axis_index("exp")
+    rows, half = tmpl_ref.shape
+    has_up = me > 0
+    has_down = me < count - 1
+
+    def copy(src, dst, n, stripe, exp):
+        return pltpu.make_async_remote_copy(
+            src_ref=src,
+            dst_ref=dst,
+            send_sem=send_sem.at[n],
+            recv_sem=recv_sem.at[n],
+            device_id={"stripe": stripe, "exp": exp},
+            device_id_type=MESH,
+        )
+
+    def sends(way, stripe, tile):
+        base = 5 * way
+        return [
+            copy(edge_send.at[way], edge_recv.at[way], base, stripe, core),
+            copy(extra_send.at[way], extra_recv.at[2 * way], base + 1, stripe, core),
+            copy(extra_send.at[way], extra_recv.at[2 * way + 1], base + 2, stripe, 1 - core),
+            copy(tile, parts.at[2 * way], base + 3, stripe, core),
+            copy(tile, parts.at[2 * way + 1], base + 4, stripe, 1 - core),
+        ]
+
+    def downs():
+        return sends(0, me + 1, tmpl_ref.at[rows - TILE : rows])
+
+    def ups():
+        return sends(1, me - 1, tmpl_ref.at[0:TILE])
+
+    more = HALF + 1 - TILE
+    extra_send[0] = tmpl_ref[rows - TILE - more : rows - TILE, :]
+    extra_send[1] = tmpl_ref[TILE : TILE + more, :]
+    edge_send[0, 0:1, :] = exp_ref[rows - 1 : rows, :]
+    edge_send[0, 1:2, :] = mask_ref[rows - 1 : rows, :].astype(jnp.float32)
+    edge_send[1, 0:1, :] = exp_ref[0:1, :]
+    edge_send[1, 1:2, :] = mask_ref[0:1, :].astype(jnp.float32)
+    barrier = pltpu.get_barrier_semaphore()
+
+    def greet(stripe, exp):
+        pl.semaphore_signal(barrier, inc=1, device_id={"stripe": stripe, "exp": exp}, device_id_type=MESH)
+
+    @pl.when(has_up)
+    def _():
+        greet(me - 1, core)
+        greet(me - 1, 1 - core)
+
+    @pl.when(has_down)
+    def _():
+        greet(me + 1, core)
+        greet(me + 1, 1 - core)
+
+    greet(me, 1 - core)
+    for partner in partners:
+        greet(partner, core)
+    pl.semaphore_wait(barrier, 1 + len(partners) + 2 * has_up.astype(jnp.int32) + 2 * has_down.astype(jnp.int32))
+
+    @pl.when(has_down)
+    def _():
+        for c in downs()[::-1]:
+            c.start()
+
+    @pl.when(has_up)
+    def _():
+        for c in ups()[::-1]:
+            c.start()
+
+    across = copy(tmpl_ref, whole, 10, me, 1 - core)
+    across.start()
+    ext_ref[...] = jnp.zeros_like(ext_ref)
+    edge_ref[...] = jnp.zeros_like(edge_ref)
+    mine = pl.ds(pl.multiple_of(EDGE + core * half, EDGE), half)
+    theirs = pl.ds(pl.multiple_of(EDGE + (1 - core) * half, EDGE), half)
+    ext_ref[rows : 2 * rows, mine] = tmpl_ref[...]
+    across.wait()
+    ext_ref[rows : 2 * rows, theirs] = whole[...]
+
+    @pl.when(has_up)
+    def _():
+        for c in downs()[1:]:
+            c.wait_recv()
+        for n, lanes in enumerate((mine, theirs)):
+            ext_ref[rows - TILE : rows, lanes] = parts[n]
+            ext_ref[rows - TILE - more : rows - TILE, lanes] = extra_recv[n]
+
+    @pl.when(has_down)
+    def _():
+        for c in ups()[1:]:
+            c.wait_recv()
+        for n, lanes in enumerate((mine, theirs)):
+            ext_ref[2 * rows : 2 * rows + TILE, lanes] = parts[2 + n]
+            ext_ref[2 * rows + TILE : 2 * rows + TILE + more, lanes] = extra_recv[2 + n]
+
+    def finish():
+        @pl.when(has_up)
+        def _():
+            downs()[0].wait_recv()
+            edge_ref[0] = edge_recv[0]
+            for c in ups():
+                c.wait_send()
+
+        @pl.when(has_down)
+        def _():
+            ups()[0].wait_recv()
+            edge_ref[1] = edge_recv[1]
+            for c in downs():
+                c.wait_send()
+
+    return finish
+
+
+def fit_kernel(
+    count,
+    fit,
+    region_rows,
+    tmpl_ref,
+    exp_ref,
+    mask_ref,
+    blk_ref,
+    rowf_ref,
+    colf_ref,
+    out_ref,
+    ext_ref,
+    edge_ref,
+    parts,
+    whole,
+    extra_send,
+    extra_recv,
+    edge_send,
+    edge_recv,
+    halo_send,
+    halo_recv,
+    local_ref,
+    bandw,
+    vert,
+    design,
+    send,
+    held,
+    send_sem,
+    recv_sem,
+):
     me = lax.axis_index("stripe")
     steps = []
     d = 1
@@ -146,10 +291,26 @@
         steps.append(d)
         d *= 2
     partners = [me + d * (1 - 2 * ((me // d) % 2)) for d in steps]
-    barrier = pltpu.get_barrier_semaphore()
-    for partner in partners:
-        pl.semaphore_signal(barrier, inc=1, device_id={"stripe": partner}, device_id_type=MESH)
-    pl.semaphore_wait(barrier, len(partners))
+    finish = exchange_halo(
+        count,
+        partners,
+        tmpl_ref,
+        exp_ref,
+        mask_ref,
+        ext_ref,
+        edge_ref,
+        parts,
+        whole,
+        extra_send,
+        extra_recv,
+        edge_send,
+        edge_recv,
+        halo_send,
+        halo_recv,
+    )
+    normal_kernel(
+        region_rows, ext_ref, exp_ref, mask_ref, blk_ref, rowf_ref, colf_ref, local_ref, bandw, vert, design
+    )
     total = local_ref[...]
     for s, partner in enumerate(partners):
         source = local_ref
@@ -169,20 +330,27 @@
         total = total + held[s]
     a = total[:fit, :]
     sub = lax.broadcasted_iota(jnp.int32, a.shape, 0)
-    for k in range(fit):
-        row = a[k : k + 1, :]
-        row = row * pl.reciprocal(jnp.broadcast_to(a[k : k + 1, k : k + 1], row.shape))
-        a = jnp.where(sub == k, row, a - a[:, k : k + 1] * row)
+    for first in range(0, fit, BLOCK):
+        block = range(first, min(first + BLOCK, fit))
+        cols = [jnp.broadcast_to(a[:, k : k + 1], a.shape) for k in block]
+        for t, k in enumerate(block):
+            inverse = pl.reciprocal(cols[t][k : k + 1, :])
+            row = a[k : k + 1, :] * inverse
+            a = jnp.where(sub == k, row, a - cols[t] * row)
+            for w in range(t + 1, len(block)):
+                factor = cols[w][k : k + 1, :] * inverse
+                cols[w] = jnp.where(sub == k, factor, cols[w] - cols[t] * factor)
     answer = jnp.broadcast_to(a[:, fit : fit + 1], a.shape)
     out_ref[...] = jnp.zeros_like(out_ref)
     out_ref[:fit, :] = answer
-
-
-def model_kernel(region_rows, coef_ref, ext_ref, exp_ref, mask_ref, rowf_ref, colf_ref, out_ref, row_ref, band, wide_y, diff):
+    finish()
+
+
+def model_kernel(region_rows, coef_ref, ext_ref, exp_ref, mask_ref, edge_ref, rowf_ref, colf_ref, out_ref, row_ref, band, wide_y, diff):
     rows, cols = out_ref.shape
     bases, taps = rowf_ref.shape
     fit = 3 * bases + 7
-    tall = exp_ref.shape[0]
+    tall = diff.shape[0]
     answer = coef_ref[:fit, :fit]
     same = lax.broadcasted_iota(jnp.int32, (fit, fit), 0) == lax.broadcasted_iota(jnp.int32, (fit, fit), 1)
     row_ref[...] = jnp.sum(jnp.where(same, answer, 0.0), axis=0, keepdims=True)
@@ -225,8 +393,12 @@
     for j in range(taps):
         y = wide_y[j * tall : (j + 1) * tall, :]
         model = model + pltpu.roll(y, wide - (EDGE - HALF) - j, 1)[:, :cols]
-    d = mask_ref[...] * (exp_ref[...] - model)
-    diff[...] = d
+    spare = jnp.zeros((tall - rows - 2, cols), jnp.float32)
+    science = jnp.concatenate([edge_ref[0, 0:1, :], exp_ref[...], edge_ref[1, 0:1, :], spare], axis=0)
+    good = jnp.concatenate(
+        [edge_ref[0, 1:2, :], mask_ref[...].astype(jnp.float32), edge_ref[1, 1:2, :], spare], axis=0
+    )
+    diff[...] = good * (science - model)
     lane = lax.broadcasted_iota(jnp.int32, (rows, cols), 1)
     mid = diff[1 : rows + 1, :]
     left = jnp.where(lane == 0, 0.0, pltpu.roll(mid, 1, 1))
@@ -239,63 +411,53 @@
     rows, cols = exposure.shape[1:]
     bases, taps = row_filters.shape
     fit = 3 * bases + 7
-    reach = HALF + 1
     stripes = lax.axis_size("stripe")
     region_rows = rows * stripes
-    me_exp = lax.axis_index("exp")
-    other = lax.ppermute(template, "exp", [(0, 1), (1, 0)])
-    is_first = me_exp == 0
-    full = jnp.concatenate([jnp.where(is_first, template, other), jnp.where(is_first, other, template)], axis=1)
     own_exp = exposure[0]
-    own_mask = cosmic_mask[0].astype(jnp.float32)
-    down = [(i, i + 1) for i in range(stripes - 1)]
-    up = [(i + 1, i) for i in range(stripes - 1)]
-    above = lax.ppermute(jnp.concatenate([full[rows - reach :], own_exp[rows - 1 :], own_mask[rows - 1 :]]), "stripe", down)
-    below = lax.ppermute(jnp.concatenate([full[:reach], own_exp[:1], own_mask[:1]]), "stripe", up)
-    side = round_up(reach, 16)
-    ext_rows = rows + 2 * side
-    ext = jnp.concatenate([above[:reach], full, below[:reach]], axis=0)
-    ext = jnp.pad(ext, ((side - reach, side - reach), (EDGE, EDGE)))
-    wide = ext.shape[1]
+    own_mask = cosmic_mask[0]
+    half = template.shape[1]
+    ext_rows = 3 * rows
+    wide = cols + 2 * EDGE
     tall = round_up(rows + 2, 8)
-    spare = jnp.zeros((tall - rows - 2, cols), jnp.float32)
-    exp_tall = jnp.concatenate([above[reach : reach + 1], own_exp, below[reach : reach + 1], spare])
-    mask_tall = jnp.concatenate([above[reach + 1 :], own_mask, below[reach + 1 :], spare])
     total = round_up(fit + 1, 8)
     vmem = pl.BlockSpec(memory_space=pltpu.VMEM)
     smem = pl.BlockSpec(memory_space=pltpu.SMEM)
     f32 = jnp.float32
-    normal = pl.pallas_call(
-        functools.partial(normal_kernel, float(region_rows)),
-        out_shape=jax.ShapeDtypeStruct((total, EDGE), f32),
+    hops = max(1, (stripes - 1).bit_length())
+    coef, ext, edges = pl.pallas_call(
+        functools.partial(fit_kernel, stripes, fit, float(region_rows)),
+        out_shape=(
+            jax.ShapeDtypeStruct((total, EDGE), f32),
+            jax.ShapeDtypeStruct((ext_rows, wide), f32),
+            jax.ShapeDtypeStruct((2, 2, cols), f32),
+        ),
         in_specs=[vmem] * 3 + [smem] + [vmem] * 2,
-        out_specs=vmem,
+        out_specs=(vmem, vmem, vmem),
         scratch_shapes=[
+            pltpu.VMEM((4, TILE, half), f32),
+            pltpu.VMEM((rows, half), f32),
+            pltpu.VMEM((2, HALF + 1 - TILE, half), f32),
+            pltpu.VMEM((4, HALF + 1 - TILE, half), f32),
+            pltpu.VMEM((2, 2, cols), f32),
+            pltpu.VMEM((2, 2, cols), f32),
+            pltpu.SemaphoreType.DMA((11,)),
+            pltpu.SemaphoreType.DMA((11,)),
+            pltpu.VMEM((total, EDGE), f32),
             pltpu.VMEM((bases * rows, 2 * EDGE), f32),
             pltpu.VMEM((bases * rows, cols), f32),
             pltpu.VMEM((cols // (2 * EDGE), total * rows, EDGE), f32),
-        ],
-        name="normal",
-    )(ext, own_exp, cosmic_mask[0], stamp_blocks, row_filters, col_filters)
-    hops = max(1, (stripes - 1).bit_length())
-    coef = pl.pallas_call(
-        functools.partial(solve_kernel, stripes, fit),
-        out_shape=jax.ShapeDtypeStruct((total, EDGE), f32),
-        in_specs=[vmem],
-        out_specs=vmem,
-        scratch_shapes=[
             pltpu.VMEM((hops, total, EDGE), f32),
             pltpu.VMEM((hops, total, EDGE), f32),
             pltpu.SemaphoreType.DMA((hops,)),
             pltpu.SemaphoreType.DMA((hops,)),
         ],
         compiler_params=pltpu.CompilerParams(collective_id=0, has_side_effects=True),
-        name="solve",
-    )(normal)
+        name="fit",
+    )(template, own_exp, own_mask, stamp_blocks, row_filters, col_filters)
     filtered, coef_row = pl.pallas_call(
         functools.partial(model_kernel, float(region_rows)),
         out_shape=(jax.ShapeDtypeStruct((rows, cols), f32), jax.ShapeDtypeStruct((1, fit), f32)),
-        in_specs=[vmem] * 6,
+        in_specs=[vmem] * 7,
         out_specs=(vmem, vmem),
         scratch_shapes=[
             pltpu.VMEM((taps * tall, EDGE), f32),
@@ -303,7 +465,7 @@
             pltpu.VMEM((tall, cols), f32),
         ],
         name="model",
-    )(coef, ext, exp_tall, mask_tall, row_filters, col_filters)
+    )(coef, ext, own_exp, own_mask, edges, row_filters, col_filters)
     return (filtered[None], coef_row)
 
 

time: 48.3 us -> 32.1 us (0.66)
  starting transfers between devices: 6.26 us -> 0 us
  waiting for transfers between devices: 6.12 us -> 0 us
  other arithmetic: 2.7 us -> 0 us
  local copies, waits for them, and re-layouts: 1.02 us -> 0 us
    ppermute x3 -> x0, starting transfers between devices: 6.26 us -> none  [the longest x1 4.41 us: shards(): lax.ppermute(jnp.concatenate([full[rows - reach:], own_exp[rows - 1:], ow...]
    ppermute x3 -> x0, waiting for transfers between devices: 6.12 us -> none  [the longest x1 4.16 us: shards(): lax.ppermute(jnp.concatenate([full[:reach], own_exp[:1], own_mask[:1]]),...]
    concatenate x5 -> x0, other arithmetic: 1.74 us -> none  [the longest x1 0.86 us: shards(): jnp.concatenate([above[reach + 1:], own_mask, below[reach + 1:], spare])]
    convert_element_type x1 -> x0, other arithmetic: 0.95 us -> none  [shards(): own_mask = cosmic_mask[0].astype(jnp.float32)]
    slice x4 -> x0, local copies, waits for them, and re-layouts: 0.93 us -> none  [the longest x1 0.88 us: shards(): own_exp[rows - 1:]]
    pallas_call x2 -> x1, Pallas kernels: 26.4 us -> 26.5 us  [shards(): pl.pallas_call(functools.partial(fit_kernel, stripes, fit, float(region_r...]
  transfers between devices with their start and end apart: 3 -> 0, of which waited for: 2 -> 0; matrix products, arithmetic and copies ran while one was open for 4% -> 0% of each run, Pallas kernels for 0% -> 0%
where the time goes in v5:
time: 32.1 us; the launch traced here: 31.9 us
  Pallas kernels  31.3 us (98%)
  between operations  0.64 us (2%)
    pallas_call x1, Pallas kernels, shards(): pl.pallas_call(functools.partial(fit_kernel, stripes, fit, float(region_r...  26.5 us
    pallas_call x1, Pallas kernels, shards(): pl.pallas_call(functools.partial(model_kernel, float(region_rows)), out_s...  4.77 us

profile of v5, /device:TPU:0, one launch (start us, length us, event | category | flops | bytes accessed | tf_op | source)
XLA Modules:
  0.0 31.9 jit_solution(12089512219509834087)
XLA Ops:
  0.6 26.5 %fit.1 = (f32[72,128]{1,0:T(8,128)}, f32[48,2304]{1,0:T(8,128)}, f32[2,2,2048]{2,1,0:T(2,128)}) custom-call(f32[16,1024]{1,0:T(8,128)} %tmpl_ref.1, f32[16,2048]{1,0:T(8,128)} %bitcast.3, s32[16,2048]{1,0:T(8,128)} %bitcast.5, s32[1,16]{1,0:T(1,128)} %blk_ref.1, f32[19,19]{1,0:T(8,128)} %rowf_ref.3, f32[19,19]{1,0:T(8,128)} %colf_ref.3), custom_call_target="tpu_custom_call" | custom-call | tf_op jit(solution)/shard_map/fit/pallas_call | solution.py:427
  27.2 4.8 %model.1 = (f32[16,2048]{1,0:T(8,128)}, f32[1,64]{1,0:T(1,128)}) custom-call(f32[72,128]{1,0:T(8,128)} %get-tuple-element.7.coef_ref, f32[48,2304]{1,0:T(8,128)} %get-tuple-element.8.ext_ref, f32[16,2048]{1,0:T(8,128)} %bitcast.4, s32[16,2048]{1,0:T(8,128)} %bitcast.6, f32[2,2,2048]{2,1,0:T(2,128)} %get-tuple-element.9.edge_ref, f32[19,19]{1,0:T(8,128)} %rowf_ref.3, ...), custom_call_target="tpu_custom_call" | custom-call | tf_op jit(solution)/shard_map/model/pallas_call | solution.py:457
